TPU v7x, 128 devices: a whole 4x4x4 slice. The times are simulated.
128 devices in a mesh: face: 4 (over y), sub: 32 (over x, z, core).
Axes of the slice: x: 4, y: 4, z: 4, core: 2. Of those that a mesh axis runs over, the one named last changes fastest.
Arguments:
- field: bfloat16 [3, 4, 128, 128, 256], P(None, 'face', 'sub'), may hold values from -6 to 6
- dw_kernel: float32 [9, 256], replicated, may hold values from -2 to 2
- dw_bias: float32 [256], replicated, may hold values from -3 to 3
- zonal_kernel: float32 [7, 256], replicated, may hold values from -2 to 2
- zonal_bias: float32 [256], replicated, may hold values from -3 to 3
- norm_gain: float32 [256], replicated, may hold values from 0.1 to 1.9
- w_in: bfloat16 [256, 768], replicated, may hold values from -0.375 to 0.375
- w_out: bfloat16 [768, 256], replicated, may hold values from -0.21875 to 0.21875
- layer_scale: float32 [256], replicated, may hold values from 0.5 to 1.5
Outputs:
- output: bfloat16 [3, 4, 128, 128, 256], P(None, 'face', 'sub')
All inputs are finite; a program needn't handle non-finite values.
Results may differ from a plain program's by a relative error of at most 0.001.
The roundings to bfloat16 on the way count: a program that leaves them out, or rounds other values in their place, can miss the bound.
Values may be sent and summed in bfloat16 or wider, within the bound.
A program may use at most 64 MiB of HBM per device.

v0:
```python
import jax
import jax.numpy as jnp
from jax import lax
from jax.sharding import PartitionSpec as P

TAPS = 7
DILATION = 4


def extended_2(block, sides, width, periodic):
    for axis, dim in sides:
        count = lax.axis_size(axis)
        forward = [(i, i + 1) for i in range(count - 1)]
        if periodic:
            forward.append((count - 1, 0))
        backward = [(target, source) for source, target in forward]
        low = lax.ppermute(
            lax.slice_in_dim(block, block.shape[dim] - width, None, axis=dim), axis, forward
        )
        high = lax.ppermute(lax.slice_in_dim(block, 0, width, axis=dim), axis, backward)
        block = jnp.concatenate([low, block, high], axis=dim)
    return block


def cut_along(value, dim, size):
    before, after = (value.shape[:dim], value.shape[dim + 1 :])
    return jnp.moveaxis(value.reshape(*before, size, -1, *after), dim, 0)


def sum_at_owner(value, axis, dim):
    parts = cut_along(value, dim, lax.axis_size(axis))
    arrived = lax.all_to_all(parts, axis, split_axis=0, concat_axis=0, tiled=True)
    return arrived.astype(jnp.float32).sum(axis=0)


def joined_along(parts, dim):
    dims = list(parts.shape[1:])
    dims[dim] *= parts.shape[0]
    return jnp.moveaxis(parts, 0, dim).reshape(dims)


def copy_for_each(value, axis):
    size = lax.axis_size(axis)
    return lax.all_to_all(
        jnp.broadcast_to(value[None], (size, *value.shape)), axis, 0, 0, tiled=True
    )


def gathered_copies(value, axis, dim):
    return joined_along(copy_for_each(value, axis), dim)


def cycle_place(facet, column, row_pos, side):
    cycle = (facet + 2) * side - column - row_pos - 1
    along = jnp.where(
        facet == 0,
        column + cycle - side,
        jnp.where((facet == 1) & (cycle < 2 * side), column + cycle - 2 * side, column),
    )
    arc_len = jnp.minimum(jnp.minimum(cycle, side), 4 * side - cycle)
    return (cycle, along, arc_len)


def cycle_cell(cycle, along, side):
    north = (cycle < 2 * side) & (along >= cycle - side)
    middle = jnp.logical_not(north) & (along < 3 * side - cycle)
    facet = jnp.where(north, jnp.int32(0), jnp.where(middle, jnp.int32(1), jnp.int32(2)))
    column = jnp.where(
        north,
        along - cycle + side,
        jnp.where(middle & (cycle < 2 * side), along + 2 * side - cycle, along),
    )
    row_pos = (facet + 2) * side - 1 - cycle - column
    return (facet, column, row_pos)


def take_row(segment_block, permutation):
    return jnp.take(segment_block, permutation, axis=2)


def reorder(values, order):
    return jax.vmap(take_row, in_axes=(1, 0), out_axes=1)(values, order)


def shards(
    field, dw_kernel, dw_bias, zonal_kernel, zonal_bias, norm_gain, w_in, w_out, layer_scale
):
    local_field = field[:, 0]
    rows_here = local_field.shape[1]
    side_cells = local_field.shape[2]
    channels = local_field.shape[3]
    edge_index = side_cells - 1
    sub_count = lax.axis_size("sub")
    quad_total = lax.axis_size("face")
    sub_index = lax.axis_index("sub")
    quad_index = lax.axis_index("face")
    row_start = sub_index * rows_here
    side_pair = jnp.stack([local_field[1, :, 0], local_field[2, :, edge_index]])
    beside_all = extended_2(side_pair, (("face", 0),), 1, True)
    last_lines = jnp.where(
        sub_index == sub_count - 1, local_field[:, rows_here - 1], jnp.zeros_like(local_field[:, 0])
    )
    first_lines = jnp.where(sub_index == 0, local_field[:, 0], jnp.zeros_like(local_field[:, 0]))
    rim_lines = jnp.swapaxes(jnp.concatenate([last_lines, first_lines], 0), 0, 1)
    pieces = sum_at_owner(rim_lines.astype(jnp.float32).astype(jnp.bfloat16), "sub", 0).astype(
        jnp.bfloat16
    )
    strips = jnp.stack(
        [
            pieces[:, 0],
            pieces[:, 1],
            local_field[2, :, 0],
            pieces[:, 5],
            local_field[0, :, edge_index],
            pieces[:, 3],
        ]
    )
    near = extended_2(strips, (("face", 0),), 3, True)
    wanted = jnp.stack([near[10], pieces[:, 2], near[11], near[1], near[2], pieces[:, 4]])
    lines = gathered_copies(wanted, "sub", 1)
    left_slice = near[0]
    right_slice = near[9]
    face_top = lines[0:3]
    face_bottom = lines[3:6]
    left_side = jnp.stack([local_field[1, :, edge_index], beside_all[0], left_slice])
    right_side = jnp.stack([right_slice, local_field[0, :, 0], beside_all[3]])
    widened = jnp.concatenate([left_side[:, :, None], local_field, right_side[:, :, None]], 2)
    extended = extended_2(widened, (("sub", 1),), 1, False)
    corner = jnp.zeros((3, 1, channels), local_field.dtype)
    face_top = jnp.concatenate([corner, face_top, corner], 1)
    face_bottom = jnp.concatenate([corner, face_bottom, corner], 1)
    first_row = jnp.where(sub_index == 0, face_top, extended[:, 0])
    final_row = jnp.where(sub_index == sub_count - 1, face_bottom, extended[:, rows_here + 1])
    padded = jnp.concatenate(
        [first_row[:, None], extended[:, 1 : rows_here + 1], final_row[:, None]], 1
    )
    total = jnp.zeros((3, rows_here, side_cells, channels), jnp.float32) + dw_bias
    for i in range(3):
        for j in range(3):
            total = total + dw_kernel[3 * i + j] * padded[
                :, i : i + rows_here, j : j + side_cells
            ].astype(jnp.float32)
    mixed = total.astype(jnp.bfloat16)
    shard_count = quad_total * sub_count
    shard_id = quad_index * sub_count + sub_index
    blocks = side_cells // shard_count
    row_ids = row_start + lax.broadcasted_iota(jnp.int32, (rows_here, shard_count), 0)
    shard_ids = lax.broadcasted_iota(jnp.int32, (rows_here, shard_count), 1)
    order = (-row_ids - 1 - shard_ids) % shard_count
    sending = reorder(mixed.reshape(3, rows_here, blocks, shard_count, channels), order)
    arrived = lax.all_to_all(sending, ("face", "sub"), split_axis=3, concat_axis=3, tiled=True)
    buffer = arrived.reshape(3, rows_here, blocks, quad_total, sub_count, channels)
    shape_out = (3, rows_here, blocks, quad_total, sub_count)
    facet = lax.broadcasted_iota(jnp.int32, shape_out, 0)
    row_local = lax.broadcasted_iota(jnp.int32, shape_out, 1)
    block_ids = lax.broadcasted_iota(jnp.int32, shape_out, 2)
    quad_out = lax.broadcasted_iota(jnp.int32, shape_out, 3)
    sub_source = lax.broadcasted_iota(jnp.int32, shape_out, 4)
    row_pos = sub_source * rows_here + row_local
    residue = (-row_pos - 1 - shard_id) % shard_count
    column = shard_count * block_ids + residue
    cycle, along, arc_len = cycle_place(facet, column, row_pos, side_cells)
    place = quad_out * arc_len + along
    flat = buffer.reshape(-1, channels)
    half = TAPS // 2
    accum = jnp.zeros(shape_out + (channels,), jnp.float32) + zonal_bias
    for k in range(TAPS):
        moved = (place + DILATION * (k - half)) % (4 * arc_len)
        quad_new = moved // arc_len
        along_new = moved % arc_len
        facet_new, column_new, row_new = cycle_cell(cycle, along_new, side_cells)
        index = (
            ((facet_new * rows_here + row_new % rows_here) * blocks + column_new // shard_count)
            * quad_total
            + quad_new
        ) * sub_count + row_new // rows_here
        gathered = jnp.take(flat, index.reshape(-1), axis=0).reshape(shape_out + (channels,))
        accum = accum + zonal_kernel[k] * gathered.astype(jnp.float32)
    zonal = accum.astype(jnp.bfloat16)
    returned = lax.all_to_all(
        zonal.reshape(3, rows_here, blocks, shard_count, channels),
        ("face", "sub"),
        split_axis=3,
        concat_axis=3,
        tiled=True,
    )
    restored = reorder(returned, order).reshape(3, rows_here, side_cells, channels)

    def finish(pair):
        zonal_face, input_face = pair
        values = zonal_face.reshape(-1, channels).astype(jnp.float32)
        mean = jnp.mean(values, -1, keepdims=True)
        spread = jnp.mean(jnp.square(values - mean), -1, keepdims=True)
        normed = ((values - mean) * lax.rsqrt(spread + 1e-06) * norm_gain).astype(jnp.bfloat16)
        hidden = jax.nn.gelu(
            jnp.dot(normed, w_in, preferred_element_type=jnp.float32), approximate=False
        ).astype(jnp.bfloat16)
        branch = jnp.dot(hidden, w_out, preferred_element_type=jnp.float32)
        source = input_face.reshape(-1, channels).astype(jnp.float32)
        result = (source + layer_scale * branch).astype(jnp.bfloat16)
        return result.reshape(rows_here, side_cells, channels)

    output = lax.map(finish, (restored, local_field))
    return output[:, None]


def solution(mesh):
    in_specs = (P(None, "face", "sub", None, None), P(), P(), P(), P(), P(), P(), P(), P())
    out_specs = P(None, "face", "sub", None, None)
    return jax.shard_map(shards, mesh=mesh, in_specs=in_specs, out_specs=out_specs, check_vma=False)
```

profile of v0, /device:TPU:1, one launch (start us, length us, event | category | flops | bytes accessed | tf_op | source)
XLA Modules:
  0.0 164.4 jit_solution(5760792183229900761)
XLA Ops:
  2.1 9.4 %all-to-all-start = ((bf16[32,4,6,256]{3,1,2,0:T(4,128)(2,1)}), bf16[32,4,6,256]{3,1,2,0:T(4,128)(2,1)S(1)}, u32[]{:S(2)}, u32[]{:S(2)}) async-start(bf16[32,4,6,256]{3,1,2,0:T(4,128)(2,1)} %copy.316), calls=%async_computation | async-start | bytes 786432 | tf_op jit(solution)/shard_map/all_to_all | solution.py:32
  11.6 2.8 %collective-permute-start.3 = (bf16[1,4,256]{2,1,0:T(4,128)(2,1)S(1)}, bf16[1,4,256]{2,1,0:T(4,128)(2,1)S(1)}, u32[]{:S(2)}, u32[]{:S(2)}) collective-permute-start(bf16[1,4,256]{2,1,0:T(4,128)(2,1)S(1)} %bitcast.200), channel_id=1, source_target_pairs={{32,0},{64,32},{96,64},{0,96},{33,1},{65,33},{97,65},{1,97},{34,2}... | collective-permute-start | bytes 6152 | tf_op jit(solution)/shard_map/ppermute | solution.py:20
  15.7 6.1 %all-to-all-done = bf16[32,4,6,256]{3,1,2,0:T(4,128)(2,1)S(1)} async-done(((bf16[32,4,6,256]{3,1,2,0:T(4,128)(2,1)}), bf16[32,4,6,256]{3,1,2,0:T(4,128)(2,1)S(1)}, u32[]{:S(2)}, u32[]{:S(2)}) %all-to-all-start) | async-done | bytes 393248 | tf_op jit(solution)/shard_map/all_to_all | solution.py:32
  22.0 2.8 %collective-permute-start = (bf16[3,4,256]{2,1,0:T(4,128)(2,1)S(1)}, bf16[3,4,256]{2,1,0:T(4,128)(2,1)S(1)}, u32[]{:S(2)}, u32[]{:S(2)}) collective-permute-start(bf16[3,4,256]{2,1,0:T(4,128)(2,1)S(1)} %pad_maximum_fusion.10), channel_id=1, source_target_pairs={{32,0},{64,32},{96,64},{0,96},{33,1},{65,33},{97,65},{1,97},{34,2}... | collective-permute-start | bytes 18440 | tf_op jit(solution)/shard_map/ppermute | solution.py:20
  25.6 3.0 %collective-permute-done.1 = bf16[3,4,256]{2,1,0:T(4,128)(2,1)S(1)} collective-permute-done((bf16[3,4,256]{2,1,0:T(4,128)(2,1)S(1)}, bf16[3,4,256]{2,1,0:T(4,128)(2,1)S(1)}, u32[]{:S(2)}, u32[]{:S(2)}) %collective-permute-start.1) | collective-permute-done | bytes 6176 | tf_op jit(solution)/shard_map/ppermute | solution.py:17
  29.5 5.0 %all-to-all-start.1 = ((bf16[32,6,4,256]{3,2,1,0:T(4,128)(2,1)}), bf16[32,6,4,256]{3,2,1,0:T(4,128)(2,1)S(1)}, u32[]{:S(2)}, u32[]{:S(2)}) async-start(bf16[32,6,4,256]{3,2,1,0:T(4,128)(2,1)} %broadcast_in_dim.92), calls=%async_computation.1 | async-start | bytes 786432 | tf_op jit(solution)/shard_map/all_to_all | solution.py:44
  34.8 3.5 %collective-permute-start.4 = (bf16[3,1,130,256]{3,2,1,0:T(8,128)(2,1)S(1)}, bf16[3,1,130,256]{3,2,1,0:T(8,128)(2,1)S(1)}, u32[]{:S(2)}, u32[]{:S(2)}) collective-permute-start(bf16[3,1,130,256]{3,2,1,0:T(8,128)(2,1)S(1)} %get-tuple-element.174), channel_id=1, source_target_pairs={{0,1},{1,2},{2,3},{3,4},{4,5},{5,6},{6,7},{7,8},{8,9},{9,10},{10,1... | collective-permute-start | bytes 599048 | tf_op jit(solution)/shard_map/ppermute | solution.py:17
  40.3 4.5 %all-to-all-done.1 = bf16[32,6,4,256]{3,2,1,0:T(4,128)(2,1)S(1)} async-done(((bf16[32,6,4,256]{3,2,1,0:T(4,128)(2,1)}), bf16[32,6,4,256]{3,2,1,0:T(4,128)(2,1)S(1)}, u32[]{:S(2)}, u32[]{:S(2)}) %all-to-all-start.1) | async-done | bytes 393248 | tf_op jit(solution)/shard_map/all_to_all | solution.py:44
  49.4 2.8 %gather_fusion = bf16[512,3,256]{2,1,0:T(4,128)(2,1)S(1)} fusion(bf16[4,3,128,256]{3,1,2,0:T(4,128)(2,1)S(1)} %copy.325, s32[512]{0:T(512)S(1)} %fusion.195), kind=kCustom, calls=%fused_computation.clone | custom fusion | bytes 1576960 | tf_op jit(solution)/shard_map/vmap(jit(_take))/gather | solution.py:78
  53.9 7.8 %all-to-all-start.2 = ((bf16[3,4,1,128,256]{4,1,2,0,3:T(4,128)(2,1)}), bf16[3,4,1,128,256]{4,1,2,0,3:T(4,128)(2,1)S(1)}, u32[]{:S(2)}, u32[]{:S(2)}) async-start(bf16[3,4,1,128,256]{4,1,2,0,3:T(4,128)(2,1)} %fusion.85), calls=%async_computation.2 | async-start | bytes 1572864 | tf_op jit(solution)/shard_map/all_to_all | solution.py:151
  63.5 14.5 %all-to-all-done.2 = bf16[3,4,1,128,256]{4,1,2,0,3:T(4,128)(2,1)S(1)} async-done(((bf16[3,4,1,128,256]{4,1,2,0,3:T(4,128)(2,1)}), bf16[3,4,1,128,256]{4,1,2,0,3:T(4,128)(2,1)S(1)}, u32[]{:S(2)}, u32[]{:S(2)}) %all-to-all-start.2) | async-done | bytes 786464 | tf_op jit(solution)/shard_map/all_to_all | solution.py:151
  78.1 5.4 %gather_fusion.2 = bf16[1536,256]{1,0:T(8,128)(2,1)} fusion(bf16[1536,256]{1,0:T(8,128)(2,1)S(1)} %bitcast.153, s32[2048]{0:T(1024)S(1)} %get-tuple-element.227), kind=kCustom, calls=%fused_computation.3.clone | custom fusion | bytes 1579008 | tf_op jit(solution)/shard_map/jit(_take)/gather | solution.py:177
  83.5 5.3 %gather_fusion.3 = bf16[1536,256]{1,0:T(8,128)(2,1)} fusion(bf16[1536,256]{1,0:T(8,128)(2,1)S(1)} %bitcast.154, s32[2048]{0:T(1024)S(1)} %get-tuple-element.226), kind=kCustom, calls=%fused_computation.4.clone | custom fusion | bytes 1579008 | tf_op jit(solution)/shard_map/jit(_take)/gather | solution.py:177
  88.8 5.4 %gather_fusion.4 = bf16[1536,256]{1,0:T(8,128)(2,1)} fusion(bf16[1536,256]{1,0:T(8,128)(2,1)S(1)} %bitcast.155, s32[2048]{0:T(1024)S(1)} %get-tuple-element.225), kind=kCustom, calls=%fused_computation.5.clone | custom fusion | bytes 1579008 | tf_op jit(solution)/shard_map/jit(_take)/gather | solution.py:177
  94.2 5.3 %gather_fusion.5 = bf16[1536,256]{1,0:T(8,128)(2,1)} fusion(bf16[1536,256]{1,0:T(8,128)(2,1)S(1)} %bitcast.156, s32[2048]{0:T(1024)S(1)} %get-tuple-element.224), kind=kCustom, calls=%fused_computation.6.clone | custom fusion | bytes 1579008 | tf_op jit(solution)/shard_map/jit(_take)/gather | solution.py:177
  99.5 5.4 %gather_fusion.6 = bf16[1536,256]{1,0:T(8,128)(2,1)} fusion(bf16[1536,256]{1,0:T(8,128)(2,1)S(1)} %bitcast.157, s32[2048]{0:T(1024)S(1)} %get-tuple-element.223), kind=kCustom, calls=%fused_computation.7.clone | custom fusion | bytes 1579008 | tf_op jit(solution)/shard_map/jit(_take)/gather | solution.py:177
  104.9 4.8 %gather_fusion.1 = bf16[1536,256]{1,0:T(8,128)(2,1)S(1)} fusion(bf16[1536,256]{1,0:T(8,128)(2,1)S(1)} %bitcast.158, s32[2048]{0:T(1024)S(1)} %pad_clamp_fusion.6), kind=kCustom, calls=%fused_computation.1.clone | custom fusion | bytes 1579008 | tf_op jit(solution)/shard_map/jit(_take)/gather | solution.py:177
  109.7 4.8 %gather_fusion.7 = bf16[1536,256]{1,0:T(8,128)(2,1)S(1)} fusion(bf16[1536,256]{1,0:T(8,128)(2,1)S(1)} %bitcast.159, s32[2048]{0:T(1024)S(1)} %get-tuple-element.222), kind=kCustom, calls=%fused_computation.8.clone | custom fusion | bytes 1579008 | tf_op jit(solution)/shard_map/jit(_take)/gather | solution.py:177
  122.4 4.7 %all-to-all-start.3 = ((bf16[3,4,1,128,256]{4,1,2,0,3:T(4,128)(2,1)}), bf16[3,4,1,128,256]{4,1,2,0,3:T(4,128)(2,1)S(1)}, u32[]{:S(2)}, u32[]{:S(2)}) async-start(bf16[3,4,1,128,256]{4,1,2,0,3:T(4,128)(2,1)} %copy.328), calls=%async_computation.3 | async-start | bytes 1572864 | tf_op jit(solution)/shard_map/all_to_all | solution.py:180
  127.1 16.4 %all-to-all-done.3 = bf16[3,4,1,128,256]{4,1,2,0,3:T(4,128)(2,1)S(1)} async-done(((bf16[3,4,1,128,256]{4,1,2,0,3:T(4,128)(2,1)}), bf16[3,4,1,128,256]{4,1,2,0,3:T(4,128)(2,1)S(1)}, u32[]{:S(2)}, u32[]{:S(2)}) %all-to-all-start.3) | async-done | bytes 786464 | tf_op jit(solution)/shard_map/all_to_all | solution.py:180
  147.4 17.1 %while.10 = (s32[]{:T(128)}, bf16[3,4,128,256]{3,2,1,0:T(8,128)(2,1)}, bf16[3,4,128,256]{3,2,1,0:T(8,128)(2,1)S(1)}, f32[256]{0:T(256)S(1)}, bf16[3,4,128,256]{3...) while((s32[]{:T(128)}, ...), condition=%wide.region_4.7_spmd, body=%wide.region_1.6_spmd.sunk | while | flops 430178816 | bytes 6838949 | solution.py:203
  148.5 3.8 %fusion.214 = bf16[512,256]{1,0:T(8,128)(2,1)S(1)} fusion(bf16[768,256]{1,0:T(8,128)(2,1)S(1)} %copy-done.11, bf16[512,256]{1,0:T(8,128)(2,1)S(1)} %fusion.213, bf16[256,768]{1,0:T(8,128)(2,1)S(1)} %copy-done.10, bf16[512,256]{1,0:T(8,128)(2,1)S(1)} %bitcast.167, f32[256]{0:T(256)S(1)} %get-tuple-element.302), kind=kOutput, calls=%fused_computation.30.clone.1 | convolution fusion | flops 428736512 | bytes 1573888 | tf_op jit(solution)/shard_map/while/body/eval_jaxpr/dot_general | solution.py:198
  154.2 3.8 %fusion.214 = bf16[512,256]{1,0:T(8,128)(2,1)S(1)} fusion(bf16[768,256]{1,0:T(8,128)(2,1)S(1)} %copy-done.11, bf16[512,256]{1,0:T(8,128)(2,1)S(1)} %fusion.213, bf16[256,768]{1,0:T(8,128)(2,1)S(1)} %copy-done.10, bf16[512,256]{1,0:T(8,128)(2,1)S(1)} %bitcast.167, f32[256]{0:T(256)S(1)} %get-tuple-element.302), kind=kOutput, calls=%fused_computation.30.clone.1 | convolution fusion | flops 428736512 | bytes 1573888 | tf_op jit(solution)/shard_map/while/body/eval_jaxpr/dot_general | solution.py:198
  159.9 3.8 %fusion.214 = bf16[512,256]{1,0:T(8,128)(2,1)S(1)} fusion(bf16[768,256]{1,0:T(8,128)(2,1)S(1)} %copy-done.11, bf16[512,256]{1,0:T(8,128)(2,1)S(1)} %fusion.213, bf16[256,768]{1,0:T(8,128)(2,1)S(1)} %copy-done.10, bf16[512,256]{1,0:T(8,128)(2,1)S(1)} %bitcast.167, f32[256]{0:T(256)S(1)} %get-tuple-element.302), kind=kOutput, calls=%fused_computation.30.clone.1 | convolution fusion | flops 428736512 | bytes 1573888 | tf_op jit(solution)/shard_map/while/body/eval_jaxpr/dot_general | solution.py:198
  (140 shorter events, 32.7 us)
Async XLA Ops:
  1.1 10.4 %copy-start = (bf16[3,1,4,128,256]{4,3,2,1,0:T(8,128)(2,1)S(1)}, bf16[3,1,4,128,256]{4,3,2,1,0:T(8,128)(2,1)}, u32[]{:S(2)}) copy-start(bf16[3,1,4,128,256]{4,3,2,1,0:T(8,128)(2,1)} %param.15) | copy-start | bytes 2359300
  1.1 13.4 %copy-start.7 = (f32[9,256]{1,0:T(8,128)S(1)}, f32[9,256]{1,0:T(8,128)}, u32[]{:S(2)}) copy-start(f32[9,256]{1,0:T(8,128)} %param.16) | copy-start | bytes 27652
  2.1 19.7 %all-to-all-start = ((bf16[32,4,6,256]{3,1,2,0:T(4,128)(2,1)}), bf16[32,4,6,256]{3,1,2,0:T(4,128)(2,1)S(1)}, u32[]{:S(2)}, u32[]{:S(2)}) async-start(bf16[32,4,6,256]{3,1,2,0:T(4,128)(2,1)} %copy.316), calls=%async_computation | async-start | bytes 786432 | tf_op jit(solution)/shard_map/all_to_all | solution.py:32
  11.6 23.0 %collective-permute-start.3 = (bf16[1,4,256]{2,1,0:T(4,128)(2,1)S(1)}, bf16[1,4,256]{2,1,0:T(4,128)(2,1)S(1)}, u32[]{:S(2)}, u32[]{:S(2)}) collective-permute-start(bf16[1,4,256]{2,1,0:T(4,128)(2,1)S(1)} %bitcast.200), channel_id=1, source_target_pairs={{32,0},{64,32},{96,64},{0,96},{33,1},{65,33},{97,65},{1,97},{34,2}... | collective-permute-start | bytes 6152 | tf_op jit(solution)/shard_map/ppermute | solution.py:20
  14.4 20.3 %collective-permute-start.2 = (bf16[1,4,256]{2,1,0:T(4,128)(2,1)S(1)}, bf16[1,4,256]{2,1,0:T(4,128)(2,1)S(1)}, u32[]{:S(2)}, u32[]{:S(2)}) collective-permute-start(bf16[1,4,256]{2,1,0:T(4,128)(2,1)S(1)} %bitcast.199), channel_id=1, source_target_pairs={{0,32},{32,64},{64,96},{96,0},{1,33},{33,65},{65,97},{97,1},{2,34}... | collective-permute-start | bytes 6152 | tf_op jit(solution)/shard_map/ppermute | solution.py:17
  22.0 3.6 %collective-permute-start = (bf16[3,4,256]{2,1,0:T(4,128)(2,1)S(1)}, bf16[3,4,256]{2,1,0:T(4,128)(2,1)S(1)}, u32[]{:S(2)}, u32[]{:S(2)}) collective-permute-start(bf16[3,4,256]{2,1,0:T(4,128)(2,1)S(1)} %pad_maximum_fusion.10), channel_id=1, source_target_pairs={{32,0},{64,32},{96,64},{0,96},{33,1},{65,33},{97,65},{1,97},{34,2}... | collective-permute-start | bytes 18440 | tf_op jit(solution)/shard_map/ppermute | solution.py:20
  24.8 3.8 %collective-permute-start.1 = (bf16[3,4,256]{2,1,0:T(4,128)(2,1)S(1)}, bf16[3,4,256]{2,1,0:T(4,128)(2,1)S(1)}, u32[]{:S(2)}, u32[]{:S(2)}) collective-permute-start(bf16[3,4,256]{2,1,0:T(4,128)(2,1)S(1)} %pad_maximum_fusion.11), channel_id=1, source_target_pairs={{0,32},{32,64},{64,96},{96,0},{1,33},{33,65},{65,97},{97,1},{2,34}... | collective-permute-start | bytes 18440 | tf_op jit(solution)/shard_map/ppermute | solution.py:17
  29.5 15.3 %all-to-all-start.1 = ((bf16[32,6,4,256]{3,2,1,0:T(4,128)(2,1)}), bf16[32,6,4,256]{3,2,1,0:T(4,128)(2,1)S(1)}, u32[]{:S(2)}, u32[]{:S(2)}) async-start(bf16[32,6,4,256]{3,2,1,0:T(4,128)(2,1)} %broadcast_in_dim.92), calls=%async_computation.1 | async-start | bytes 786432 | tf_op jit(solution)/shard_map/all_to_all | solution.py:44
  34.8 10.3 %collective-permute-start.4 = (bf16[3,1,130,256]{3,2,1,0:T(8,128)(2,1)S(1)}, bf16[3,1,130,256]{3,2,1,0:T(8,128)(2,1)S(1)}, u32[]{:S(2)}, u32[]{:S(2)}) collective-permute-start(bf16[3,1,130,256]{3,2,1,0:T(8,128)(2,1)S(1)} %get-tuple-element.174), channel_id=1, source_target_pairs={{0,1},{1,2},{2,3},{3,4},{4,5},{5,6},{6,7},{7,8},{8,9},{9,10},{10,1... | collective-permute-start | bytes 599048 | tf_op jit(solution)/shard_map/ppermute | solution.py:17
  38.4 7.2 %collective-permute-start.5 = (bf16[3,1,130,256]{3,2,1,0:T(8,128)(2,1)S(1)}, bf16[3,1,130,256]{3,2,1,0:T(8,128)(2,1)S(1)}, u32[]{:S(2)}, u32[]{:S(2)}) collective-permute-start(bf16[3,1,130,256]{3,2,1,0:T(8,128)(2,1)S(1)} %get-tuple-element.175), channel_id=1, source_target_pairs={{1,0},{2,1},{3,2},{4,3},{5,4},{6,5},{7,6},{8,7},{9,8},{10,9},{11,1... | collective-permute-start | bytes 599048 | tf_op jit(solution)/shard_map/ppermute | solution.py:20
  53.9 9.5 %copy-start.6 = (f32[7,256]{1,0:T(8,128)S(1)}, f32[7,256]{1,0:T(8,128)}, u32[]{:S(2)}) copy-start(f32[7,256]{1,0:T(8,128)} %param.18) | copy-start | bytes 21508
  53.9 24.1 %all-to-all-start.2 = ((bf16[3,4,1,128,256]{4,1,2,0,3:T(4,128)(2,1)}), bf16[3,4,1,128,256]{4,1,2,0,3:T(4,128)(2,1)S(1)}, u32[]{:S(2)}, u32[]{:S(2)}) async-start(bf16[3,4,1,128,256]{4,1,2,0,3:T(4,128)(2,1)} %fusion.85), calls=%async_computation.2 | async-start | bytes 1572864 | tf_op jit(solution)/shard_map/all_to_all | solution.py:151
  114.4 1.5 copy-start.4
  115.9 1.1 copy-start.2
  116.2 1.2 copy-start.3
  117.3 1.2 copy-start.1
  122.4 21.1 %all-to-all-start.3 = ((bf16[3,4,1,128,256]{4,1,2,0,3:T(4,128)(2,1)}), bf16[3,4,1,128,256]{4,1,2,0,3:T(4,128)(2,1)S(1)}, u32[]{:S(2)}, u32[]{:S(2)}) async-start(bf16[3,4,1,128,256]{4,1,2,0,3:T(4,128)(2,1)} %copy.328), calls=%async_computation.3 | async-start | bytes 1572864 | tf_op jit(solution)/shard_map/all_to_all | solution.py:180
  146.7 0.7 copy-start.12
  147.4 1.0 copy-start.10
  147.4 1.1 copy-start.11
  153.1 1.0 copy-start.10
  153.1 1.1 copy-start.11
  158.8 1.0 copy-start.10
  158.8 1.1 copy-start.11
  (3 other events, 2.0 us)
where the time goes:
time: 165 us; the launch traced here: 164 us
  local copies, waits for them, and re-layouts  54.2 us (33%)
  waiting for transfers between devices  45.5 us (28%)
  starting transfers between devices  38.1 us (23%)
  other arithmetic  14.4 us (9%)
  matrix products  11.5 us (7%)
    gather x7, local copies, waits for them, and re-layouts, shards(): jnp.take(flat, index.reshape(-1), axis=0).reshape(shape_out + (channels,))  36.3 us
    all_to_all x1, waiting for transfers between devices, shards(): lax.all_to_all(zonal.reshape(3, rows_here, blocks, shard_count, channels)...  16.4 us
    all_to_all x1, waiting for transfers between devices, shards(): lax.all_to_all(sending, ('face', 'sub'), split_axis=3, concat_axis=3, til...  14.5 us
    dot_general x3, matrix products, finish(): branch = jnp.dot(hidden, w_out, preferred_element_type=jnp.float32)  11.5 us
    all_to_all x1, starting transfers between devices, sum_at_owner(): lax.all_to_all(parts, axis, split_axis=0, concat_axis=0, tiled=True)  9.42 us
    all_to_all x1, starting transfers between devices, shards(): lax.all_to_all(sending, ('face', 'sub'), split_axis=3, concat_axis=3, til...  7.84 us
    ppermute x3, starting transfers between devices, extended_2(): lax.ppermute(lax.slice_in_dim(block, 0, width, axis=dim), axis, backward)  7.53 us
    all_to_all x1, waiting for transfers between devices, sum_at_owner(): lax.all_to_all(parts, axis, split_axis=0, concat_axis=0, tiled=True)  6.07 us
  transfers between devices with their start and end apart: 10, of which 7 were waited for; matrix products, arithmetic and copies ran while one was open for 3% of the time, Pallas kernels for 0%

commit v1 on v0

v1 whole, which is shorter than its diff:
```python
import functools

import jax
import jax.numpy as jnp
import numpy as np
from jax import lax
from jax.experimental import pallas as pl
from jax.experimental.pallas import tpu as pltpu
from jax.sharding import PartitionSpec as P

MESH = pl.DeviceIdType.MESH
TAPS = 7
SIDE = 128
ALL = 128
LANES = 128
VP = 385
UP = 257
BASE_N = 288
LIN_ROWS = 1664
ZROWS = 1072


def place_of(index):
    return index // 32, lax.rem(index, 32)


def peer_at(face, sub, step):
    x = sub // 8
    z = lax.rem(sub // 2, 4)
    core = lax.rem(sub, 2)
    pf = lax.rem(face + lax.rem(step, 4), 4)
    px = lax.rem(x + lax.rem(step // 4, 4), 4)
    pz = lax.rem(z + lax.rem(step // 16, 4), 4)
    pc = lax.rem(core + step // 64, 2)
    return pf, px * 8 + pz * 2 + pc


def enter(face, sub):
    barrier = pltpu.get_barrier_semaphore()

    def greet(i, carry):
        pf, ps = peer_at(face, sub, ALL - i)
        pl.semaphore_signal(barrier, inc=1, device_id=(pf, ps), device_id_type=MESH)
        return carry

    lax.fori_loop(1, ALL, greet, 0)
    pl.semaphore_wait(barrier, ALL - 1)


def exchange(face, sub, me, source, target, send_sem, recv_sem):
    def issue(i, carry):
        pf, ps = peer_at(face, sub, ALL - i)
        pltpu.make_async_remote_copy(
            source.at[pf * 32 + ps],
            target.at[me],
            send_sem,
            recv_sem,
            device_id=(pf, ps),
            device_id_type=MESH,
        ).start()
        return carry

    lax.fori_loop(1, ALL, issue, 0)
    target[me] = source[me]


def settle(face, sub, source, target, send_sem, recv_sem):
    whole = pltpu.make_async_remote_copy(
        source.at[pl.ds(0, ALL - 1)],
        target.at[pl.ds(0, ALL - 1)],
        send_sem,
        recv_sem,
        device_id=(face, sub),
        device_id_type=MESH,
    )
    whole.wait_send()
    whole.wait_recv()


def kernel(
    mixed_ref, field_ref, zk_ref, zb_ref, gain_ref, w_in_ref, w_out_ref, ls_ref, out_ref,
    turned, send, recv, chain1, chain2, polar, lin, zlin, back_send, back_recv, unturned,
    send_sem, recv_sem,
):
    face = lax.axis_index("face")
    sub = lax.axis_index("sub")
    me = face * 32 + sub
    enter(face, sub)

    for f in range(3):
        for j in range(4):
            y = sub * 4 + j
            for h in range(2):
                rows = mixed_ref[f, j, :, h * LANES : (h + 1) * LANES].astype(jnp.float32)
                base = (f * 8 + j * 2 + h) * VP
                turned[pl.ds(base + y, SIDE), :] = rows
                turned[pl.ds(base + y + SIDE, SIDE), :] = rows

    def pack(c, carry):
        for f in range(3):
            cells = turned[pl.ds(f * 8 * VP + SIDE + c, 8, stride=VP), :]
            send[c, f] = cells.astype(jnp.bfloat16)
        return carry

    lax.fori_loop(0, ALL, pack, 0, unroll=8)
    exchange(face, sub, me, send, recv, send_sem.at[0], recv_sem.at[0])
    settle(face, sub, send, recv, send_sem.at[0], recv_sem.at[0])

    c = me
    row_in = lax.broadcasted_iota(jnp.int32, (8, LANES), 0) // 2

    def unpack(i, carry):
        q = i // 32
        s = lax.rem(i, 32)
        at = (3 - q) * 32 + s
        upper = row_in + 4 * s > c
        north = recv[i, 0].astype(jnp.float32)
        middle = recv[i, 1].astype(jnp.float32)
        south = recv[i, 2].astype(jnp.float32)
        chain1[at + 3] = jnp.where(upper, middle, north)
        before = recv[lax.rem(i + 96, ALL), 2].astype(jnp.float32)
        chain2[at + 3] = jnp.where(upper, before, middle)
        polar[pl.ds(pl.multiple_of(8 * i, 8), 8), :] = jnp.where(upper, north, south)
        return carry

    lax.fori_loop(0, ALL, unpack, 0, unroll=4)
    for chain in (chain1, chain2):
        for e in range(3):
            chain[e] = chain[ALL + e]
            chain[ALL + 3 + e] = chain[3 + e]

    arc_n = SIDE - 1 - c
    arc_s = c + 1
    base_s = BASE_N + 8 * arc_n + 48
    for q in range(4):
        lin[pl.ds(BASE_N + (3 - q) * 2 * arc_n - 2 * (c + 1), 256), :] = polar[
            q * 256 : (q + 1) * 256, :
        ]
    for q in (3, 2, 1, 0):
        lin[pl.ds(base_s + (3 - q) * 2 * arc_s, 256), :] = polar[q * 256 : (q + 1) * 256, :]
    for base, size in ((BASE_N, 8 * arc_n), (base_s, 8 * arc_s)):
        for e in range(3):
            lin[pl.ds(base + size + 8 * e, 8), :] = lin[pl.ds(base + 8 * e, 8), :]
        for e in range(1, 4):
            lin[pl.ds(base - 8 * e, 8), :] = lin[pl.ds(base - 8 * e + size, 8), :]

    def coeff(ref, k):
        lo = jnp.broadcast_to(ref[k : k + 1, :LANES], (8, LANES))
        hi = jnp.broadcast_to(ref[k : k + 1, LANES:], (8, LANES))
        odd = lax.rem(lax.broadcasted_iota(jnp.int32, (8, LANES), 0), 2) == 1
        return jnp.where(odd, hi, lo)

    taps = [coeff(zk_ref, k) for k in range(TAPS)]
    bias = coeff(zb_ref, 0)

    def stencil_lin(v, carry):
        at = pl.multiple_of(BASE_N + 8 * v, 8)
        total = bias
        for k in range(TAPS):
            total = total + taps[k] * lin[pl.ds(pl.multiple_of(at - 8 * (k - 3), 8), 8), :]
        zlin[pl.ds(at, 8), :] = total
        return carry

    lax.fori_loop(0, ZROWS // 8, stencil_lin, 0, unroll=2)
    row_256 = lax.broadcasted_iota(jnp.int32, (256, LANES), 0) // 2
    for q in range(4):
        from_n = zlin[pl.ds(BASE_N + (3 - q) * 2 * arc_n - 2 * (c + 1), 256), :]
        from_s = zlin[pl.ds(base_s + (3 - q) * 2 * arc_s, 256), :]
        polar[q * 256 : (q + 1) * 256, :] = jnp.where(row_256 > c, from_n, from_s)

    def finish_zonal(i, carry):
        q = i // 32
        s = lax.rem(i, 32)
        at = (3 - q) * 32 + s
        upper = row_in + 4 * s > c
        z1 = bias
        z2 = bias
        for k in range(TAPS):
            z1 = z1 + taps[k] * chain1[at + 6 - k]
            z2 = z2 + taps[k] * chain2[at + 6 - k]
        zp = polar[pl.ds(pl.multiple_of(8 * i, 8), 8), :]
        back_send[i, 0] = jnp.where(upper, zp, z1).astype(jnp.bfloat16)
        back_send[i, 1] = jnp.where(upper, z1, z2).astype(jnp.bfloat16)
        west = lax.rem(i + 96, ALL)
        zp = polar[pl.ds(pl.multiple_of(8 * west, 8), 8), :]
        back_send[west, 2] = jnp.where(upper, z2, zp).astype(jnp.bfloat16)
        return carry

    lax.fori_loop(0, ALL, finish_zonal, 0, unroll=2)
    exchange(face, sub, me, back_send, back_recv, send_sem.at[1], recv_sem.at[1])
    settle(face, sub, back_send, back_recv, send_sem.at[1], recv_sem.at[1])

    def unturn(i, carry):
        for f in range(3):
            cells = back_recv[i, f].astype(jnp.float32)
            unturned[pl.ds(f * 8 * UP + i, 8, stride=UP), :] = cells
            unturned[pl.ds(f * 8 * UP + i + SIDE, 8, stride=UP), :] = cells
        return carry

    lax.fori_loop(0, ALL, unturn, 0, unroll=8)

    gain = gain_ref[...]
    scale = ls_ref[...]
    w_in = w_in_ref[...]
    w_out = w_out_ref[...]

    def mlp(t, carry):
        f = t // 4
        j = lax.rem(t, 4)
        y = sub * 4 + j
        base = (f * 8 + j * 2) * UP + y
        values = jnp.concatenate(
            [unturned[pl.ds(base, SIDE), :], unturned[pl.ds(base + UP, SIDE), :]], axis=1
        )
        mean = jnp.mean(values, -1, keepdims=True)
        centred = values - mean
        spread = jnp.mean(jnp.square(centred), -1, keepdims=True)
        normed = (centred * lax.rsqrt(spread + 1e-06) * gain).astype(jnp.bfloat16)
        pre = jnp.dot(normed, w_in, preferred_element_type=jnp.float32)
        hidden = (0.5 * pre * (1.0 + lax.erf(pre * np.float32(np.sqrt(0.5))))).astype(jnp.bfloat16)
        branch = jnp.dot(hidden, w_out, preferred_element_type=jnp.float32)
        result = field_ref[f, j].astype(jnp.float32) + scale * branch
        out_ref[f, j] = result.astype(jnp.bfloat16)
        return carry

    lax.fori_loop(0, 12, mlp, 0)


def run(mixed, local_field, zonal_kernel, zonal_bias, norm_gain, w_in, w_out, layer_scale):
    vmem = pl.BlockSpec(memory_space=pltpu.VMEM)
    cells = pltpu.VMEM((ALL, 3, 8, LANES), jnp.bfloat16)
    return pl.pallas_call(
        kernel,
        out_shape=jax.ShapeDtypeStruct(local_field.shape, jnp.bfloat16),
        in_specs=[vmem] * 8,
        out_specs=vmem,
        scratch_shapes=[
            pltpu.VMEM((24 * VP, LANES), jnp.float32),
            cells,
            cells,
            pltpu.VMEM((ALL + 6, 8, LANES), jnp.float32),
            pltpu.VMEM((ALL + 6, 8, LANES), jnp.float32),
            pltpu.VMEM((1024, LANES), jnp.float32),
            pltpu.VMEM((LIN_ROWS, LANES), jnp.float32),
            pltpu.VMEM((LIN_ROWS, LANES), jnp.float32),
            cells,
            cells,
            pltpu.VMEM((24 * UP, LANES), jnp.float32),
            pltpu.SemaphoreType.DMA((2,)),
            pltpu.SemaphoreType.DMA((2,)),
        ],
        compiler_params=pltpu.CompilerParams(
            collective_id=0, has_side_effects=True, vmem_limit_bytes=56 * 1024 * 1024
        ),
    )(
        mixed, local_field, zonal_kernel, zonal_bias[None], norm_gain[None], w_in, w_out,
        layer_scale[None],
    )


def extended_2(block, sides, width, periodic):
    for axis, dim in sides:
        count = lax.axis_size(axis)
        forward = [(i, i + 1) for i in range(count - 1)]
        if periodic:
            forward.append((count - 1, 0))
        backward = [(target, source) for source, target in forward]
        low = lax.ppermute(
            lax.slice_in_dim(block, block.shape[dim] - width, None, axis=dim), axis, forward
        )
        high = lax.ppermute(lax.slice_in_dim(block, 0, width, axis=dim), axis, backward)
        block = jnp.concatenate([low, block, high], axis=dim)
    return block


def cut_along(value, dim, size):
    before, after = (value.shape[:dim], value.shape[dim + 1 :])
    return jnp.moveaxis(value.reshape(*before, size, -1, *after), dim, 0)


def sum_at_owner(value, axis, dim):
    parts = cut_along(value, dim, lax.axis_size(axis))
    arrived = lax.all_to_all(parts, axis, split_axis=0, concat_axis=0, tiled=True)
    return arrived.astype(jnp.float32).sum(axis=0)


def joined_along(parts, dim):
    dims = list(parts.shape[1:])
    dims[dim] *= parts.shape[0]
    return jnp.moveaxis(parts, 0, dim).reshape(dims)


def copy_for_each(value, axis):
    size = lax.axis_size(axis)
    return lax.all_to_all(
        jnp.broadcast_to(value[None], (size, *value.shape)), axis, 0, 0, tiled=True
    )


def gathered_copies(value, axis, dim):
    return joined_along(copy_for_each(value, axis), dim)


def shards(
    field, dw_kernel, dw_bias, zonal_kernel, zonal_bias, norm_gain, w_in, w_out, layer_scale
):
    local_field = field[:, 0]
    rows_here = local_field.shape[1]
    side_cells = local_field.shape[2]
    channels = local_field.shape[3]
    edge_index = side_cells - 1
    sub_count = lax.axis_size("sub")
    quad_total = lax.axis_size("face")
    sub_index = lax.axis_index("sub")
    quad_index = lax.axis_index("face")
    row_start = sub_index * rows_here
    side_pair = jnp.stack([local_field[1, :, 0], local_field[2, :, edge_index]])
    beside_all = extended_2(side_pair, (("face", 0),), 1, True)
    last_lines = jnp.where(
        sub_index == sub_count - 1, local_field[:, rows_here - 1], jnp.zeros_like(local_field[:, 0])
    )
    first_lines = jnp.where(sub_index == 0, local_field[:, 0], jnp.zeros_like(local_field[:, 0]))
    rim_lines = jnp.swapaxes(jnp.concatenate([last_lines, first_lines], 0), 0, 1)
    pieces = sum_at_owner(rim_lines.astype(jnp.float32).astype(jnp.bfloat16), "sub", 0).astype(
        jnp.bfloat16
    )
    strips = jnp.stack(
        [
            pieces[:, 0],
            pieces[:, 1],
            local_field[2, :, 0],
            pieces[:, 5],
            local_field[0, :, edge_index],
            pieces[:, 3],
        ]
    )
    near = extended_2(strips, (("face", 0),), 3, True)
    wanted = jnp.stack([near[10], pieces[:, 2], near[11], near[1], near[2], pieces[:, 4]])
    lines = gathered_copies(wanted, "sub", 1)
    left_slice = near[0]
    right_slice = near[9]
    face_top = lines[0:3]
    face_bottom = lines[3:6]
    left_side = jnp.stack([local_field[1, :, edge_index], beside_all[0], left_slice])
    right_side = jnp.stack([right_slice, local_field[0, :, 0], beside_all[3]])
    widened = jnp.concatenate([left_side[:, :, None], local_field, right_side[:, :, None]], 2)
    extended = extended_2(widened, (("sub", 1),), 1, False)
    corner = jnp.zeros((3, 1, channels), local_field.dtype)
    face_top = jnp.concatenate([corner, face_top, corner], 1)
    face_bottom = jnp.concatenate([corner, face_bottom, corner], 1)
    first_row = jnp.where(sub_index == 0, face_top, extended[:, 0])
    final_row = jnp.where(sub_index == sub_count - 1, face_bottom, extended[:, rows_here + 1])
    padded = jnp.concatenate(
        [first_row[:, None], extended[:, 1 : rows_here + 1], final_row[:, None]], 1
    )
    total = jnp.zeros((3, rows_here, side_cells, channels), jnp.float32) + dw_bias
    for i in range(3):
        for j in range(3):
            total = total + dw_kernel[3 * i + j] * padded[
                :, i : i + rows_here, j : j + side_cells
            ].astype(jnp.float32)
    mixed = total.astype(jnp.bfloat16)
    output = run(
        mixed, local_field, zonal_kernel, zonal_bias, norm_gain, w_in, w_out, layer_scale
    )
    return output[:, None]


def solution(mesh):
    in_specs = (P(None, "face", "sub", None, None), P(), P(), P(), P(), P(), P(), P(), P())
    out_specs = P(None, "face", "sub", None, None)
    return jax.shard_map(shards, mesh=mesh, in_specs=in_specs, out_specs=out_specs, check_vma=False)
```

time: 165 us -> 99.9 us (0.61)
  local copies, waits for them, and re-layouts: 54.2 us -> 4.72 us
  Pallas kernels: 0 us -> 47.2 us
  waiting for transfers between devices: 45.5 us -> 15.9 us
  starting transfers between devices: 38.1 us -> 25.6 us
  matrix products: 11.5 us -> 0 us
  other arithmetic: 14.4 us -> 5.74 us
    pallas_call x0 -> x1, Pallas kernels: none -> 47.2 us  [run(): pl.pallas_call(kernel, out_shape=jax.ShapeDtypeStruct(local_field.shape,...]
    gather x9 -> x0, local copies, waits for them, and re-layouts: 41.9 us -> none  [the longest x7 36.3 us: shards(): jnp.take(flat, index.reshape(-1), axis=0).reshape(shape_out + (channels,))]
    all_to_all x2 -> x0, waiting for transfers between devices: 30.9 us -> none  [the longest x1 16.4 us: shards(): lax.all_to_all(zonal.reshape(3, rows_here, blocks, shard_count, channels)...]
    all_to_all x2 -> x0, starting transfers between devices: 12.6 us -> none  [the longest x1 7.84 us: shards(): lax.all_to_all(sending, ('face', 'sub'), split_axis=3, concat_axis=3, til...]
    dot_general x3 -> x0, matrix products: 11.5 us -> none  [finish(): branch = jnp.dot(hidden, w_out, preferred_element_type=jnp.float32)]
    transpose x2 -> x0, other arithmetic: 3.95 us -> none  [the longest x1 2.22 us: take_row(): return jnp.take(segment_block, permutation, axis=2)]
    dynamic_update_slice x3 -> x0, local copies, waits for them, and re-layouts: 2.18 us -> none  [shards(): output = lax.map(finish, (restored, local_field))]
    select_n x7 -> x1, other arithmetic: 3.09 us -> 0.94 us  [shards(): jnp.where(sub_index == 0, local_field[:, 0], jnp.zeros_like(local_field[:...]
  transfers between devices with their start and end apart: 10 -> 8, of which waited for: 7 -> 5; matrix products, arithmetic and copies ran while one was open for 3% -> 2% of each run, Pallas kernels for 0% -> 0%
where the time goes in v1:
time: 99.9 us; the launch traced here: 99.4 us
  Pallas kernels  47.2 us (47%)
  starting transfers between devices  25.6 us (26%)
  waiting for transfers between devices  15.9 us (16%)
  other arithmetic  5.74 us (6%)
  local copies, waits for them, and re-layouts  4.72 us (5%)
    pallas_call x1, Pallas kernels, run(): pl.pallas_call(kernel, out_shape=jax.ShapeDtypeStruct(local_field.shape,...  47.2 us
    all_to_all x1, starting transfers between devices, sum_at_owner(): lax.all_to_all(parts, axis, split_axis=0, concat_axis=0, tiled=True)  9.42 us
    all_to_all x1, waiting for transfers between devices, sum_at_owner(): lax.all_to_all(parts, axis, split_axis=0, concat_axis=0, tiled=True)  7.3 us
    ppermute x3, starting transfers between devices, extended_2(): lax.ppermute(lax.slice_in_dim(block, 0, width, axis=dim), axis, backward)  6.25 us
    ppermute x3, starting transfers between devices, extended_2(): lax.ppermute(lax.slice_in_dim(block, block.shape[dim] - width, None, axis...  4.98 us
    all_to_all x1, starting transfers between devices, copy_for_each(): lax.all_to_all(jnp.broadcast_to(value[None], (size, *value.shape)), axis,...  4.97 us
    all_to_all x1, waiting for transfers between devices, copy_for_each(): lax.all_to_all(jnp.broadcast_to(value[None], (size, *value.shape)), axis,...  4.59 us
    ppermute x3, waiting for transfers between devices, extended_2(): lax.ppermute(lax.slice_in_dim(block, block.shape[dim] - width, None, axis...  2.98 us
  transfers between devices with their start and end apart: 8, of which 5 were waited for; matrix products, arithmetic and copies ran while one was open for 2% of the time, Pallas kernels for 0%

profile of v1, /device:TPU:1, one launch (start us, length us, event | category | flops | bytes accessed | tf_op | source)
XLA Modules:
  0.0 99.4 jit_solution(16540180139148312271)
XLA Ops:
  0.0 0.9 fusion.2
  0.9 1.0 fusion.4
  2.1 0.9 copy.98
  3.0 9.4 %all-to-all-start = ((bf16[32,4,6,256]{3,1,2,0:T(4,128)(2,1)}), bf16[32,4,6,256]{3,1,2,0:T(4,128)(2,1)S(1)}, u32[]{:S(2)}, u32[]{:S(2)}) async-start(bf16[32,4,6,256]{3,1,2,0:T(4,128)(2,1)} %copy.98), calls=%async_computation | async-start | bytes 786432 | tf_op jit(solution)/shard_map/all_to_all | solution.py:283
  12.4 1.4 %collective-permute-start.2 = (bf16[1,4,256]{2,1,0:T(4,128)(2,1)S(1)}, bf16[1,4,256]{2,1,0:T(4,128)(2,1)S(1)}, u32[]{:S(2)}, u32[]{:S(2)}) collective-permute-start(bf16[1,4,256]{2,1,0:T(4,128)(2,1)S(1)} %bitcast.89), channel_id=1, source_target_pairs={{0,32},{32,64},{64,96},{96,0},{1,33},{33,65},{65,97},{97,1},{2,34}... | collective-permute-start | bytes 6152 | tf_op jit(solution)/shard_map/ppermute | solution.py:268
  13.8 1.5 %collective-permute-start.3 = (bf16[1,4,256]{2,1,0:T(4,128)(2,1)S(1)}, bf16[1,4,256]{2,1,0:T(4,128)(2,1)S(1)}, u32[]{:S(2)}, u32[]{:S(2)}) collective-permute-start(bf16[1,4,256]{2,1,0:T(4,128)(2,1)S(1)} %bitcast.90), channel_id=1, source_target_pairs={{32,0},{64,32},{96,64},{0,96},{33,1},{65,33},{97,65},{1,97},{34,2}... | collective-permute-start | bytes 6152 | tf_op jit(solution)/shard_map/ppermute | solution.py:271
  15.4 7.3 %all-to-all-done = bf16[32,4,6,256]{3,1,2,0:T(4,128)(2,1)S(1)} async-done(((bf16[32,4,6,256]{3,1,2,0:T(4,128)(2,1)}), bf16[32,4,6,256]{3,1,2,0:T(4,128)(2,1)S(1)}, u32[]{:S(2)}, u32[]{:S(2)}) %all-to-all-start) | async-done | bytes 393248 | tf_op jit(solution)/shard_map/all_to_all | solution.py:283
  22.7 0.2 reduce_sum.12
  22.9 2.8 %collective-permute-start = (bf16[3,4,256]{2,1,0:T(4,128)(2,1)S(1)}, bf16[3,4,256]{2,1,0:T(4,128)(2,1)S(1)}, u32[]{:S(2)}, u32[]{:S(2)}) collective-permute-start(bf16[3,4,256]{2,1,0:T(4,128)(2,1)S(1)} %pad_maximum_fusion.10), channel_id=1, source_target_pairs={{32,0},{64,32},{96,64},{0,96},{33,1},{65,33},{97,65},{1,97},{34,2}... | collective-permute-start | bytes 18440 | tf_op jit(solution)/shard_map/ppermute | solution.py:271
  25.8 0.7 collective-permute-done
  26.5 3.0 %collective-permute-done.1 = bf16[3,4,256]{2,1,0:T(4,128)(2,1)S(1)} collective-permute-done((bf16[3,4,256]{2,1,0:T(4,128)(2,1)S(1)}, bf16[3,4,256]{2,1,0:T(4,128)(2,1)S(1)}, u32[]{:S(2)}, u32[]{:S(2)}) %collective-permute-start.1) | collective-permute-done | bytes 6176 | tf_op jit(solution)/shard_map/ppermute | solution.py:268
  29.5 0.9 broadcast_in_dim.31
  30.3 5.0 %all-to-all-start.1 = ((bf16[32,6,4,256]{3,2,1,0:T(4,128)(2,1)}), bf16[32,6,4,256]{3,2,1,0:T(4,128)(2,1)S(1)}, u32[]{:S(2)}, u32[]{:S(2)}) async-start(bf16[32,6,4,256]{3,2,1,0:T(4,128)(2,1)} %broadcast_in_dim.31), calls=%async_computation.1 | async-start | bytes 786432 | tf_op jit(solution)/shard_map/all_to_all | solution.py:295
  35.5 3.5 %collective-permute-start.4 = (bf16[3,1,130,256]{3,2,1,0:T(8,128)(2,1)S(1)}, bf16[3,1,130,256]{3,2,1,0:T(8,128)(2,1)S(1)}, u32[]{:S(2)}, u32[]{:S(2)}) collective-permute-start(bf16[3,1,130,256]{3,2,1,0:T(8,128)(2,1)S(1)} %get-tuple-element.7), channel_id=1, source_target_pairs={{0,1},{1,2},{2,3},{3,4},{4,5},{5,6},{6,7},{7,8},{8,9},{9,10},{10,1... | collective-permute-start | bytes 599048 | tf_op jit(solution)/shard_map/ppermute | solution.py:268
  39.1 1.9 %collective-permute-start.5 = (bf16[3,1,130,256]{3,2,1,0:T(8,128)(2,1)S(1)}, bf16[3,1,130,256]{3,2,1,0:T(8,128)(2,1)S(1)}, u32[]{:S(2)}, u32[]{:S(2)}) collective-permute-start(bf16[3,1,130,256]{3,2,1,0:T(8,128)(2,1)S(1)} %get-tuple-element.8), channel_id=1, source_target_pairs={{1,0},{2,1},{3,2},{4,3},{5,4},{6,5},{7,6},{8,7},{9,8},{10,9},{11,1... | collective-permute-start | bytes 599048 | tf_op jit(solution)/shard_map/ppermute | solution.py:271
  41.0 4.6 %all-to-all-done.1 = bf16[32,6,4,256]{3,2,1,0:T(4,128)(2,1)S(1)} async-done(((bf16[32,6,4,256]{3,2,1,0:T(4,128)(2,1)}), bf16[32,6,4,256]{3,2,1,0:T(4,128)(2,1)S(1)}, u32[]{:S(2)}, u32[]{:S(2)}) %all-to-all-start.1) | async-done | bytes 393248 | tf_op jit(solution)/shard_map/all_to_all | solution.py:295
  45.6 0.1 fusion.6
  46.0 0.3 collective-permute-done.5
  46.3 0.2 fusion
  46.5 0.4 maximum_maximum_fusion
  46.9 0.3 copy-done.2
  47.2 2.9 %add_convert_fusion.mixed_ref = bf16[3,4,128,256]{3,2,1,0:T(8,128)(2,1)} fusion(bf16[3,4,128,256]{3,2,1,0:T(8,128)(2,1)S(1)} %bitcast.75, bf16[3,5,130,256]{3,2,1,0:T(8,128)(2,1)S(1)} %get-tuple-element.6, bf16[3,4,1,256]{3,2,1,0:T(2,128)(2,1)S(1)} %copy.101, bf16[3,4,1,256]{3,2,1,0:T(2,128)(2,1)S(1)} %copy.100, ...), kind=kLoop, calls=%fused_computation | loop fusion | flops 13369344 | bytes 6313984 | tf_op jit(solution)/shard_map/convert_element_type | solution.py:362
  50.1 47.2 %shard_map.91 = bf16[3,4,128,256]{3,2,1,0:T(8,128)(2,1)} custom-call(bf16[3,4,128,256]{3,2,1,0:T(8,128)(2,1)} %add_convert_fusion.mixed_ref, bf16[3,4,128,256]{3,2,1,0:T(8,128)(2,1)} %bitcast.71, f32[7,256]{1,0:T(8,128)} %zk_ref.1, f32[1,256]{1,0:T(1,128)} %bitcast.91, f32[1,256]{1,0:T(1,128)} %bitcast.92, bf16[256,768]{1,0:T(8,128)(2,1)} %w_in_ref.1, ...), custom_call_target="tpu_custom_call" | custom-call | tf_op jit(solution)/shard_map/pallas_call | solution.py:232
  97.4 2.1 %copy.128 = bf16[3,1,4,128,256]{4,3,2,1,0:T(8,128)(2,1)} copy(bf16[3,1,4,128,256]{4,3,2,1,0:T(8,128)(2,1)} %bitcast.76) | data formatting | bytes 1572864
  (37 shorter events, 0.8 us)
Async XLA Ops:
  1.9 10.4 %copy-start = (bf16[3,1,4,128,256]{4,3,2,1,0:T(8,128)(2,1)S(1)}, bf16[3,1,4,128,256]{4,3,2,1,0:T(8,128)(2,1)}, u32[]{:S(2)}) copy-start(bf16[3,1,4,128,256]{4,3,2,1,0:T(8,128)(2,1)} %param.9) | copy-start | bytes 2359300
  2.0 13.4 %copy-start.1 = (f32[9,256]{1,0:T(8,128)S(1)}, f32[9,256]{1,0:T(8,128)}, u32[]{:S(2)}) copy-start(f32[9,256]{1,0:T(8,128)} %param.10) | copy-start | bytes 27652
  3.0 19.7 %all-to-all-start = ((bf16[32,4,6,256]{3,1,2,0:T(4,128)(2,1)}), bf16[32,4,6,256]{3,1,2,0:T(4,128)(2,1)S(1)}, u32[]{:S(2)}, u32[]{:S(2)}) async-start(bf16[32,4,6,256]{3,1,2,0:T(4,128)(2,1)} %copy.98), calls=%async_computation | async-start | bytes 786432 | tf_op jit(solution)/shard_map/all_to_all | solution.py:283
  12.4 22.9 %collective-permute-start.2 = (bf16[1,4,256]{2,1,0:T(4,128)(2,1)S(1)}, bf16[1,4,256]{2,1,0:T(4,128)(2,1)S(1)}, u32[]{:S(2)}, u32[]{:S(2)}) collective-permute-start(bf16[1,4,256]{2,1,0:T(4,128)(2,1)S(1)} %bitcast.89), channel_id=1, source_target_pairs={{0,32},{32,64},{64,96},{96,0},{1,33},{33,65},{65,97},{97,1},{2,34}... | collective-permute-start | bytes 6152 | tf_op jit(solution)/shard_map/ppermute | solution.py:268
  13.8 21.5 %collective-permute-start.3 = (bf16[1,4,256]{2,1,0:T(4,128)(2,1)S(1)}, bf16[1,4,256]{2,1,0:T(4,128)(2,1)S(1)}, u32[]{:S(2)}, u32[]{:S(2)}) collective-permute-start(bf16[1,4,256]{2,1,0:T(4,128)(2,1)S(1)} %bitcast.90), channel_id=1, source_target_pairs={{32,0},{64,32},{96,64},{0,96},{33,1},{65,33},{97,65},{1,97},{34,2}... | collective-permute-start | bytes 6152 | tf_op jit(solution)/shard_map/ppermute | solution.py:271
  22.9 3.6 %collective-permute-start = (bf16[3,4,256]{2,1,0:T(4,128)(2,1)S(1)}, bf16[3,4,256]{2,1,0:T(4,128)(2,1)S(1)}, u32[]{:S(2)}, u32[]{:S(2)}) collective-permute-start(bf16[3,4,256]{2,1,0:T(4,128)(2,1)S(1)} %pad_maximum_fusion.10), channel_id=1, source_target_pairs={{32,0},{64,32},{96,64},{0,96},{33,1},{65,33},{97,65},{1,97},{34,2}... | collective-permute-start | bytes 18440 | tf_op jit(solution)/shard_map/ppermute | solution.py:271
  25.7 3.8 %collective-permute-start.1 = (bf16[3,4,256]{2,1,0:T(4,128)(2,1)S(1)}, bf16[3,4,256]{2,1,0:T(4,128)(2,1)S(1)}, u32[]{:S(2)}, u32[]{:S(2)}) collective-permute-start(bf16[3,4,256]{2,1,0:T(4,128)(2,1)S(1)} %pad_maximum_fusion.11), channel_id=1, source_target_pairs={{0,32},{32,64},{64,96},{96,0},{1,33},{33,65},{65,97},{97,1},{2,34}... | collective-permute-start | bytes 18440 | tf_op jit(solution)/shard_map/ppermute | solution.py:268
  30.3 15.3 %all-to-all-start.1 = ((bf16[32,6,4,256]{3,2,1,0:T(4,128)(2,1)}), bf16[32,6,4,256]{3,2,1,0:T(4,128)(2,1)S(1)}, u32[]{:S(2)}, u32[]{:S(2)}) async-start(bf16[32,6,4,256]{3,2,1,0:T(4,128)(2,1)} %broadcast_in_dim.31), calls=%async_computation.1 | async-start | bytes 786432 | tf_op jit(solution)/shard_map/all_to_all | solution.py:295
  35.5 10.5 %collective-permute-start.4 = (bf16[3,1,130,256]{3,2,1,0:T(8,128)(2,1)S(1)}, bf16[3,1,130,256]{3,2,1,0:T(8,128)(2,1)S(1)}, u32[]{:S(2)}, u32[]{:S(2)}) collective-permute-start(bf16[3,1,130,256]{3,2,1,0:T(8,128)(2,1)S(1)} %get-tuple-element.7), channel_id=1, source_target_pairs={{0,1},{1,2},{2,3},{3,4},{4,5},{5,6},{6,7},{7,8},{8,9},{9,10},{10,1... | collective-permute-start | bytes 599048 | tf_op jit(solution)/shard_map/ppermute | solution.py:268
  39.1 7.3 %collective-permute-start.5 = (bf16[3,1,130,256]{3,2,1,0:T(8,128)(2,1)S(1)}, bf16[3,1,130,256]{3,2,1,0:T(8,128)(2,1)S(1)}, u32[]{:S(2)}, u32[]{:S(2)}) collective-permute-start(bf16[3,1,130,256]{3,2,1,0:T(8,128)(2,1)S(1)} %get-tuple-element.8), channel_id=1, source_target_pairs={{1,0},{2,1},{3,2},{4,3},{5,4},{6,5},{7,6},{8,7},{9,8},{10,9},{11,1... | collective-permute-start | bytes 599048 | tf_op jit(solution)/shard_map/ppermute | solution.py:271
  46.5 0.7 copy-start.2

commit v2 on v1

v2 whole, which is shorter than its diff:
```python
import functools

import jax
import jax.numpy as jnp
import numpy as np
from jax import lax
from jax.experimental import pallas as pl
from jax.experimental.pallas import tpu as pltpu
from jax.sharding import PartitionSpec as P

MESH = pl.DeviceIdType.MESH
TAPS = 7
SIDE = 128
ALL = 128
LANES = 128
PITCH = 137
ROW = 8
TURN = 137
FACE_ROWS = 8 * TURN + 16
BASE_N = 288
LIN_ROWS = 1664
ZROWS = 1072


def place_of(index):
    return index // 32, lax.rem(index, 32)


def peer_at(face, sub, step):
    x = sub // 8
    z = lax.rem(sub // 2, 4)
    core = lax.rem(sub, 2)
    pf = lax.rem(face + lax.rem(step, 4), 4)
    px = lax.rem(x + lax.rem(step // 4, 4), 4)
    pz = lax.rem(z + lax.rem(step // 16, 4), 4)
    pc = lax.rem(core + step // 64, 2)
    return pf, px * 8 + pz * 2 + pc


def announce(face, sub):
    barrier = pltpu.get_barrier_semaphore()

    def greet(i, carry):
        pf, ps = peer_at(face, sub, ALL - i)
        pl.semaphore_signal(barrier, inc=1, device_id=(pf, ps), device_id_type=MESH)
        return carry

    lax.fori_loop(1, ALL, greet, 0)


def exchange(face, sub, me, source, target, send_sem, recv_sem):
    def issue(i, carry):
        pf, ps = peer_at(face, sub, ALL - i)
        pltpu.make_async_remote_copy(
            source.at[pf * 32 + ps],
            target.at[me],
            send_sem,
            recv_sem,
            device_id=(pf, ps),
            device_id_type=MESH,
        ).start()
        return carry

    lax.fori_loop(1, ALL, issue, 0)
    target[me] = source[me]


def settle(face, sub, source, target, send_sem, recv_sem):
    whole = pltpu.make_async_remote_copy(
        source.at[pl.ds(0, ALL - 1)],
        target.at[pl.ds(0, ALL - 1)],
        send_sem,
        recv_sem,
        device_id=(face, sub),
        device_id_type=MESH,
    )
    whole.wait_send()
    whole.wait_recv()


def kernel(
    field_ref, dwk_ref, dwb_ref, zk_ref, zb_ref, gain_ref, w_in_ref, w_out_ref, ls_ref, out_ref,
    grid, row_lo, row_hi, cols, left1, right2, pieces, right0, left2, rim_hi, rim_lo, rim_rows,
    turned, send, recv, chain1, chain2, polar, lin, zlin, back_send, back_recv,
    send_sem, recv_sem, row_sent, lo_sem, hi_sem, col_sent, left_sem, right_sem, piece_sent,
    piece_sem, rim_sent, rim_sem,
):
    face = lax.axis_index("face")
    sub = lax.axis_index("sub")
    me = face * 32 + sub
    east = lax.rem(face + 1, 4)
    west = lax.rem(face + 3, 4)
    first = sub == 0
    last = sub == 31
    announce(face, sub)

    def start(f, r, h=0):
        return (f * 12 + r * 2 + h) * PITCH + ROW

    def widen(t, carry):
        f = t // 4
        j = lax.rem(t, 4)
        for h in range(2):
            grid[pl.ds(start(f, j + 1, h), SIDE), :] = field_ref[
                f, j, :, h * LANES : (h + 1) * LANES
            ].astype(jnp.float32)
        return carry

    lax.fori_loop(0, 12, widen, 0)
    for n, (f, x) in enumerate(((2, SIDE - 1), (1, 0), (0, SIDE - 1), (2, 0))):
        cols[n] = grid[pl.ds(start(f, 1) + x, 8, stride=PITCH), :].astype(jnp.bfloat16)

    def cut(base):
        def one(t, carry):
            for h in range(2):
                at = base + h * PITCH + 4 * t - 1
                pieces[t, h] = grid[pl.ds(at, 8), :].astype(jnp.bfloat16)
            return carry

        lax.fori_loop(0, 32, one, 0)

    pl.when(last)(lambda: cut(start(0, 4)))
    pl.when(first)(lambda: cut(start(2, 1)))

    def push(source, target, sent, got, pf, ps):
        return pltpu.make_async_remote_copy(
            source, target, sent, got, device_id=(pf, ps), device_id_type=MESH
        )

    inner = []
    for f in range(3):
        inner.append((sub < 31, push(
            field_ref.at[f, 3], row_lo.at[f], row_sent.at[0, f], lo_sem.at[f], face, sub + 1)))
        inner.append((sub > 0, push(
            field_ref.at[f, 0], row_hi.at[f], row_sent.at[1, f], hi_sem.at[f], face, sub - 1)))
    inner.append((last, push(
        field_ref.at[1, 3], row_lo.at[0], row_sent.at[0, 1], lo_sem.at[0], west, 0)))
    inner.append((last, push(
        field_ref.at[2, 3], row_lo.at[1], row_sent.at[0, 2], lo_sem.at[1], face, 0)))
    inner.append((first, push(
        field_ref.at[0, 0], row_hi.at[1], row_sent.at[1, 0], hi_sem.at[1], east, 31)))
    inner.append((first, push(
        field_ref.at[1, 0], row_hi.at[2], row_sent.at[1, 1], hi_sem.at[2], face, 31)))
    for d, cond in ((-1, sub > 0), (0, sub >= 0), (1, sub < 31)):
        inner.append((cond, push(
            cols.at[0], left1.at[1 - d], col_sent.at[0, 1 - d], left_sem.at[1 - d], east, sub + d)))
        inner.append((cond, push(
            cols.at[1], right2.at[1 - d], col_sent.at[1, 1 - d], right_sem.at[1 - d], west, sub + d)))
    inner.append((sub >= 0, push(
        cols.at[2], rim_hi.at[sub], rim_sent.at[0], rim_sem.at[0], east, 31)))
    inner.append((sub >= 0, push(
        cols.at[3], rim_lo.at[sub], rim_sent.at[1], rim_sem.at[1], west, 0)))

    pl.semaphore_wait(pltpu.get_barrier_semaphore(), ALL - 1)
    for cond, copy in inner:
        pl.when(cond)(copy.start)

    def scatter(pf, target, got):
        def one(t, carry):
            push(pieces.at[t], target, piece_sent, got, pf, t).start()
            return carry

        lax.fori_loop(0, 32, one, 0)

    pl.when(last)(lambda: scatter(west, right0, piece_sem.at[0]))
    pl.when(first)(lambda: scatter(east, left2, piece_sem.at[1]))

    def weight(ref, tap, h):
        return ref[tap : tap + 1, h * LANES : (h + 1) * LANES]

    def partial_sum(total, f, j, h, x, size, rows):
        for i in rows:
            for k in range(3):
                at = start(f, j + i, h) + x + k - 1
                total = total + weight(dwk_ref, 3 * i + k, h) * grid[pl.ds(at, size), :]
        return total

    def slot(f, j, h):
        return f * FACE_ROWS + (2 * j + h) * TURN + j + 8

    def inside(f, carry):
        for j in range(4):
            rows = (1, 2) if j == 0 else (0, 1) if j == 3 else (0, 1, 2)
            for h in range(2):
                for x in (8, 64):
                    zero = jnp.broadcast_to(weight(dwb_ref, 0, h), (56, LANES))
                    turned[pl.ds(slot(f, j, h) + x, 56), :] = partial_sum(
                        zero, f, j, h, x, 56, rows)
        return carry

    lax.fori_loop(0, 3, inside, 0)

    def took(ref, sem):
        push(ref, ref, row_sent.at[0, 0], sem, face, sub).wait_recv()

    for f in range(3):
        pl.when((sub > 0) if f == 2 else (sub >= 0))(
            lambda f=f: took(row_lo.at[f], lo_sem.at[f]))
        pl.when((sub < 31) if f == 0 else (sub >= 0))(
            lambda f=f: took(row_hi.at[f], hi_sem.at[f]))
    took(right0, piece_sem.at[0])
    took(left2, piece_sem.at[1])
    for e, cond in ((0, sub > 0), (1, sub >= 0), (2, sub < 31)):
        pl.when(cond)(lambda e=e: took(left1.at[e], left_sem.at[e]))
        pl.when(cond)(lambda e=e: took(right2.at[e], right_sem.at[e]))

    for f in range(3):
        for h in range(2):
            half = slice(h * LANES, (h + 1) * LANES)
            grid[pl.ds(start(f, 0, h), SIDE), :] = row_lo[f, :, half].astype(jnp.float32)
            grid[pl.ds(start(f, 5, h), SIDE), :] = row_hi[f, :, half].astype(jnp.float32)

    def rim(ref, sem, f, r):
        took(ref, sem)
        rim_rows[...] = ref[...].astype(jnp.float32).reshape(2 * SIDE, LANES)
        for h in range(2):
            grid[pl.ds(start(f, r, h), SIDE), :] = rim_rows[pl.ds(h, SIDE, stride=2), :]

    pl.when(first)(lambda: rim(rim_lo, rim_sem.at[1], 2, 0))
    pl.when(last)(lambda: rim(rim_hi, rim_sem.at[0], 0, 5))

    for r, size in ((0, 8), (4, 4)):
        grid[pl.ds(start(0, r) - 1, size, stride=PITCH), :] = grid[
            pl.ds(start(1, r) + SIDE - 1, size, stride=PITCH), :]
        grid[pl.ds(start(1, r) + SIDE, size, stride=PITCH), :] = grid[
            pl.ds(start(0, r), size, stride=PITCH), :]
    for f, x, ref in ((1, -1, left1), (2, SIDE, right2)):
        before = ref[0].astype(jnp.float32)
        after = ref[2].astype(jnp.float32)
        grid[pl.ds(start(f, 0) + x, 2, stride=PITCH), :] = before[6:8]
        grid[pl.ds(start(f, 1) + x, 8, stride=PITCH), :] = ref[1].astype(jnp.float32)
        grid[pl.ds(start(f, 5) + x, 2, stride=PITCH), :] = after[0:2]
    for f, x, ref in ((0, SIDE, right0), (2, -1, left2)):
        for h in range(2):
            grid[pl.ds(start(f, 0, h) + x, 6, stride=2 * PITCH), :] = ref[h].astype(jnp.float32)[:6]

    def corners(r):
        for f in range(3):
            for x in (-1, SIDE):
                grid[pl.ds(start(f, r) + x, 2, stride=PITCH), :] = jnp.zeros((2, LANES), jnp.float32)

    pl.when(first)(lambda: corners(0))
    pl.when(last)(lambda: corners(5))

    def around(f, carry):
        for j in range(4):
            for h in range(2):
                for x in (0, SIDE - 8):
                    zero = jnp.broadcast_to(weight(dwb_ref, 0, h), (8, LANES))
                    turned[pl.ds(slot(f, j, h) + x, 8), :] = partial_sum(
                        zero, f, j, h, x, 8, (0, 1, 2))
                if j in (0, 3):
                    for x in (8, 64):
                        at = pl.ds(slot(f, j, h) + x, 56)
                        turned[at, :] = partial_sum(
                            turned[at, :], f, j, h, x, 56, (0,) if j == 0 else (2,))
                if j:
                    turned[pl.ds(slot(f, j, h) - j, j), :] = turned[
                        pl.ds(slot(f, j, h) + SIDE - j, j), :]
        return carry

    lax.fori_loop(0, 3, around, 0)

    def pack(t, carry):
        c = lax.rem(t + 4 * sub, ALL)
        for f in range(3):
            cells = turned[pl.ds(f * FACE_ROWS + 8 + t, 8, stride=TURN), :]
            send[c, f] = cells.astype(jnp.bfloat16)
        return carry

    lax.fori_loop(0, ALL, pack, 0, unroll=8)
    exchange(face, sub, me, send, recv, send_sem.at[0], recv_sem.at[0])
    settle(face, sub, send, recv, send_sem.at[0], recv_sem.at[0])
    for cond, copy in inner:
        pl.when(cond)(copy.wait_send)
    pl.when(first | last)(
        lambda: push(pieces, pieces, piece_sent, piece_sem.at[0], face, sub).wait_send())

    c = me
    row_in = lax.broadcasted_iota(jnp.int32, (8, LANES), 0) // 2

    def unpack(i, carry):
        q = i // 32
        s = lax.rem(i, 32)
        at = (3 - q) * 32 + s
        upper = row_in + 4 * s > c
        north = recv[i, 0].astype(jnp.float32)
        middle = recv[i, 1].astype(jnp.float32)
        south = recv[i, 2].astype(jnp.float32)
        chain1[at + 3] = jnp.where(upper, middle, north)
        before = recv[lax.rem(i + 96, ALL), 2].astype(jnp.float32)
        chain2[at + 3] = jnp.where(upper, before, middle)
        polar[pl.ds(pl.multiple_of(8 * i, 8), 8), :] = jnp.where(upper, north, south)
        return carry

    lax.fori_loop(0, ALL, unpack, 0, unroll=4)
    for chain in (chain1, chain2):
        for e in range(3):
            chain[e] = chain[ALL + e]
            chain[ALL + 3 + e] = chain[3 + e]

    arc_n = SIDE - 1 - c
    arc_s = c + 1
    base_s = BASE_N + 8 * arc_n + 48
    for q in range(4):
        lin[pl.ds(BASE_N + (3 - q) * 2 * arc_n - 2 * (c + 1), 256), :] = polar[
            q * 256 : (q + 1) * 256, :
        ]
    for q in (3, 2, 1, 0):
        lin[pl.ds(base_s + (3 - q) * 2 * arc_s, 256), :] = polar[q * 256 : (q + 1) * 256, :]
    for base, size in ((BASE_N, 8 * arc_n), (base_s, 8 * arc_s)):
        for e in range(3):
            lin[pl.ds(base + size + 8 * e, 8), :] = lin[pl.ds(base + 8 * e, 8), :]
        for e in range(1, 4):
            lin[pl.ds(base - 8 * e, 8), :] = lin[pl.ds(base - 8 * e + size, 8), :]

    def coeff(ref, k):
        lo = jnp.broadcast_to(ref[k : k + 1, :LANES], (8, LANES))
        hi = jnp.broadcast_to(ref[k : k + 1, LANES:], (8, LANES))
        odd = lax.rem(lax.broadcasted_iota(jnp.int32, (8, LANES), 0), 2) == 1
        return jnp.where(odd, hi, lo)

    taps = [coeff(zk_ref, k) for k in range(TAPS)]
    bias = coeff(zb_ref, 0)

    def stencil_lin(v, carry):
        at = pl.multiple_of(BASE_N + 8 * v, 8)
        total = bias
        for k in range(TAPS):
            total = total + taps[k] * lin[pl.ds(pl.multiple_of(at - 8 * (k - 3), 8), 8), :]
        zlin[pl.ds(at, 8), :] = total
        return carry

    lax.fori_loop(0, ZROWS // 8, stencil_lin, 0, unroll=2)
    row_256 = lax.broadcasted_iota(jnp.int32, (256, LANES), 0) // 2
    for q in range(4):
        from_n = zlin[pl.ds(BASE_N + (3 - q) * 2 * arc_n - 2 * (c + 1), 256), :]
        from_s = zlin[pl.ds(base_s + (3 - q) * 2 * arc_s, 256), :]
        polar[q * 256 : (q + 1) * 256, :] = jnp.where(row_256 > c, from_n, from_s)

    def finish_zonal(i, carry):
        q = i // 32
        s = lax.rem(i, 32)
        at = (3 - q) * 32 + s
        upper = row_in + 4 * s > c
        z1 = bias
        z2 = bias
        for k in range(TAPS):
            z1 = z1 + taps[k] * chain1[at + 6 - k]
            z2 = z2 + taps[k] * chain2[at + 6 - k]
        zp = polar[pl.ds(pl.multiple_of(8 * i, 8), 8), :]
        back_send[i, 0] = jnp.where(upper, zp, z1).astype(jnp.bfloat16)
        back_send[i, 1] = jnp.where(upper, z1, z2).astype(jnp.bfloat16)
        back = lax.rem(i + 96, ALL)
        zp = polar[pl.ds(pl.multiple_of(8 * back, 8), 8), :]
        back_send[back, 2] = jnp.where(upper, z2, zp).astype(jnp.bfloat16)
        return carry

    lax.fori_loop(0, ALL, finish_zonal, 0, unroll=2)
    exchange(face, sub, me, back_send, back_recv, send_sem.at[1], recv_sem.at[1])
    settle(face, sub, back_send, back_recv, send_sem.at[1], recv_sem.at[1])

    def unturn(i, carry):
        t = lax.rem(i + ALL - 4 * sub, ALL)
        for f in range(3):
            turned[pl.ds(f * FACE_ROWS + 8 + t, 8, stride=TURN), :] = back_recv[i, f].astype(
                jnp.float32)
        return carry

    lax.fori_loop(0, ALL, unturn, 0, unroll=8)
    for f in range(3):
        for j in range(1, 4):
            for h in range(2):
                turned[pl.ds(slot(f, j, h) + SIDE - j, j), :] = turned[
                    pl.ds(slot(f, j, h) - j, j), :]

    gain = gain_ref[...]
    scale = ls_ref[...]
    w_in = w_in_ref[...]
    w_out = w_out_ref[...]

    def mlp(t, carry):
        f = t // 4
        j = lax.rem(t, 4)
        base = f * FACE_ROWS + 2 * j * TURN + j + 8
        values = jnp.concatenate(
            [turned[pl.ds(base, SIDE), :], turned[pl.ds(base + TURN, SIDE), :]], axis=1
        )
        mean = jnp.mean(values, -1, keepdims=True)
        centred = values - mean
        spread = jnp.mean(jnp.square(centred), -1, keepdims=True)
        normed = (centred * lax.rsqrt(spread + 1e-06) * gain).astype(jnp.bfloat16)
        pre = jnp.dot(normed, w_in, preferred_element_type=jnp.float32)
        hidden = (0.5 * pre * (1.0 + lax.erf(pre * np.float32(np.sqrt(0.5))))).astype(jnp.bfloat16)
        branch = jnp.dot(hidden, w_out, preferred_element_type=jnp.float32)
        result = field_ref[f, j].astype(jnp.float32) + scale * branch
        out_ref[f, j] = result.astype(jnp.bfloat16)
        return carry

    lax.fori_loop(0, 12, mlp, 0)


def run(field, dw_kernel, dw_bias, zonal_kernel, zonal_bias, norm_gain, w_in, w_out, layer_scale):
    vmem = pl.BlockSpec(memory_space=pltpu.VMEM)
    cells = pltpu.VMEM((ALL, 3, 8, LANES), jnp.bfloat16)
    lines = pltpu.VMEM((3, SIDE, 2 * LANES), jnp.bfloat16)
    tiles = lambda *lead: pltpu.VMEM((*lead, 8, LANES), jnp.bfloat16)
    rows = lambda n: pltpu.VMEM((n, LANES), jnp.float32)
    dma = pltpu.SemaphoreType.DMA
    return pl.pallas_call(
        kernel,
        out_shape=jax.ShapeDtypeStruct(field.shape, jnp.bfloat16),
        in_specs=[vmem] * 9,
        out_specs=vmem,
        scratch_shapes=[
            rows(36 * PITCH + 16),
            lines,
            lines,
            tiles(4),
            tiles(3),
            tiles(3),
            tiles(32, 2),
            tiles(2),
            tiles(2),
            tiles(32),
            tiles(32),
            rows(2 * SIDE),
            rows(3 * FACE_ROWS + 8),
            cells,
            cells,
            pltpu.VMEM((ALL + 6, 8, LANES), jnp.float32),
            pltpu.VMEM((ALL + 6, 8, LANES), jnp.float32),
            rows(1024),
            rows(LIN_ROWS),
            rows(LIN_ROWS),
            cells,
            cells,
            dma((2,)),
            dma((2,)),
            dma((2, 3)),
            dma((3,)),
            dma((3,)),
            dma((2, 3)),
            dma((3,)),
            dma((3,)),
            dma,
            dma((2,)),
            dma((2,)),
            dma((2,)),
        ],
        compiler_params=pltpu.CompilerParams(
            collective_id=0, has_side_effects=True, vmem_limit_bytes=56 * 1024 * 1024
        ),
    )(
        field, dw_kernel, dw_bias[None], zonal_kernel, zonal_bias[None], norm_gain[None], w_in,
        w_out, layer_scale[None],
    )


def shards(
    field, dw_kernel, dw_bias, zonal_kernel, zonal_bias, norm_gain, w_in, w_out, layer_scale
):
    output = run(
        field[:, 0], dw_kernel, dw_bias, zonal_kernel, zonal_bias, norm_gain, w_in, w_out,
        layer_scale,
    )
    return output[:, None]


def solution(mesh):
    in_specs = (P(None, "face", "sub", None, None), P(), P(), P(), P(), P(), P(), P(), P())
    out_specs = P(None, "face", "sub", None, None)
    return jax.shard_map(shards, mesh=mesh, in_specs=in_specs, out_specs=out_specs, check_vma=False)
```

time: 99.9 us -> 60.7 us (0.61)
  starting transfers between devices: 25.6 us -> 0 us
  waiting for transfers between devices: 15.9 us -> 0 us
  Pallas kernels: 47.2 us -> 58.4 us
  other arithmetic: 5.74 us -> 0 us
  local copies, waits for them, and re-layouts: 4.72 us -> 2.06 us
    all_to_all x2 -> x0, starting transfers between devices: 14.4 us -> none  [the longest x1 9.42 us: sum_at_owner(): lax.all_to_all(parts, axis, split_axis=0, concat_axis=0, tiled=True)]
    all_to_all x2 -> x0, waiting for transfers between devices: 11.9 us -> none  [the longest x1 7.3 us: sum_at_owner(): lax.all_to_all(parts, axis, split_axis=0, concat_axis=0, tiled=True)]
    ppermute x6 -> x0, starting transfers between devices: 11.2 us -> none  [the longest x3 6.25 us: extended_2(): lax.ppermute(lax.slice_in_dim(block, 0, width, axis=dim), axis, backward)]
    pallas_call x1, Pallas kernels: 47.2 us -> 58.4 us  [run(): pl.pallas_call(kernel, out_shape=jax.ShapeDtypeStruct(field.shape, jnp.bf...]
    ppermute x6 -> x0, waiting for transfers between devices: 3.97 us -> none  [the longest x3 2.98 us: extended_2(): lax.ppermute(lax.slice_in_dim(block, block.shape[dim] - width, None, axis...]
    convert_element_type x1 -> x0, other arithmetic: 2.93 us -> none  [shards(): mixed = total.astype(jnp.bfloat16)]
    select_n x3 -> x0, other arithmetic: 2.06 us -> none  [the longest x1 0.95 us: shards(): jnp.where(sub_index == sub_count - 1, local_field[:, rows_here - 1], jnp....]
    unnamed x16 -> x1, local copies, waits for them, and re-layouts: 2.42 us -> 2.06 us
  transfers between devices with their start and end apart: 8 -> 0, of which waited for: 5 -> 0; matrix products, arithmetic and copies ran while one was open for 2% -> 0% of each run, Pallas kernels for 0% -> 0%
where the time goes in v2:
time: 60.7 us; the launch traced here: 60.5 us
  Pallas kernels  58.4 us (96%)
  local copies, waits for them, and re-layouts  2.06 us (3%)
    pallas_call x1, Pallas kernels, run(): pl.pallas_call(kernel, out_shape=jax.ShapeDtypeStruct(field.shape, jnp.bf...  58.4 us
    unnamed x1, local copies, waits for them, and re-layouts  2.06 us

profile of v2, /device:TPU:1, one launch (start us, length us, event | category | flops | bytes accessed | tf_op | source)
XLA Modules:
  0.0 60.5 jit_solution(15453618219883087943)
XLA Ops:
  0.0 58.4 %shard_map.91 = bf16[3,4,128,256]{3,2,1,0:T(8,128)(2,1)} custom-call(bf16[3,4,128,256]{3,2,1,0:T(8,128)(2,1)} %bitcast.9, f32[9,256]{1,0:T(8,128)} %dwk_ref.1, f32[1,256]{1,0:T(1,128)} %bitcast.10, f32[7,256]{1,0:T(8,128)} %zk_ref.1, f32[1,256]{1,0:T(1,128)} %bitcast.11, f32[1,256]{1,0:T(1,128)} %bitcast.12, bf16[256,768]{1,0:T(8,128)(2,1)} %w_in_ref.1, ...), custom_call_target="tpu_custom_call" | custom-call | tf_op jit(solution)/shard_map/pallas_call | solution.py:410
  58.4 2.1 %copy.12 = bf16[3,1,4,128,256]{4,3,2,1,0:T(8,128)(2,1)} copy(bf16[3,1,4,128,256]{4,3,2,1,0:T(8,128)(2,1)} %bitcast.8) | data formatting | bytes 1572864

commit v3 on v2

--- a/solution.py
+++ b/solution.py
@@ -22,19 +22,12 @@
 ZROWS = 1072
 
 
-def place_of(index):
-    return index // 32, lax.rem(index, 32)
-
-
 def peer_at(face, sub, step):
-    x = sub // 8
-    z = lax.rem(sub // 2, 4)
-    core = lax.rem(sub, 2)
-    pf = lax.rem(face + lax.rem(step, 4), 4)
-    px = lax.rem(x + lax.rem(step // 4, 4), 4)
-    pz = lax.rem(z + lax.rem(step // 16, 4), 4)
-    pc = lax.rem(core + step // 64, 2)
-    return pf, px * 8 + pz * 2 + pc
+    pf = (face + step) & 3
+    px = ((sub >> 3) + (step >> 2)) & 3
+    pz = ((sub >> 1) + (step >> 4)) & 3
+    pc = (sub + (step >> 6)) & 1
+    return pf, (px << 3) + (pz << 1) + pc
 
 
 def announce(face, sub):
@@ -45,12 +38,13 @@
         pl.semaphore_signal(barrier, inc=1, device_id=(pf, ps), device_id_type=MESH)
         return carry
 
-    lax.fori_loop(1, ALL, greet, 0)
-
-
-def exchange(face, sub, me, source, target, send_sem, recv_sem):
-    def issue(i, carry):
-        pf, ps = peer_at(face, sub, ALL - i)
+    lax.fori_loop(1, ALL, greet, 0, unroll=2)
+
+
+def exchange(face, sub, prepare, source, target, send_sem, recv_sem):
+    me = face * 32 + sub
+
+    def push(pf, ps):
         pltpu.make_async_remote_copy(
             source.at[pf * 32 + ps],
             target.at[me],
@@ -59,10 +53,16 @@
             device_id=(pf, ps),
             device_id_type=MESH,
         ).start()
-        return carry
-
-    lax.fori_loop(1, ALL, issue, 0)
-    target[me] = source[me]
+
+    def step(i, carry):
+        pf, ps = peer_at(face, sub, ALL - i)
+        prepare(pf, ps)
+        push(*carry)
+        return pf, ps
+
+    pf, ps = peer_at(face, sub, ALL - 1)
+    prepare(pf, ps)
+    push(*lax.fori_loop(2, ALL, step, (pf, ps), unroll=2))
 
 
 def settle(face, sub, source, target, send_sem, recv_sem):
@@ -79,7 +79,8 @@
 
 
 def kernel(
-    field_ref, dwk_ref, dwb_ref, zk_ref, zb_ref, gain_ref, w_in_ref, w_out_ref, ls_ref, out_ref,
+    field_hbm, dwk_hbm, dwb_hbm, zk_hbm, zb_hbm, gain_hbm, w_in_hbm, w_out_hbm, ls_hbm, out_ref,
+    field_ref, dwk_ref, dwb_ref, zk_ref, zb_ref, gain_ref, w_in_ref, w_out_ref, ls_ref, load_sem,
     grid, row_lo, row_hi, cols, left1, right2, pieces, right0, left2, rim_hi, rim_lo, rim_rows,
     turned, send, recv, chain1, chain2, polar, lin, zlin, back_send, back_recv,
     send_sem, recv_sem, row_sent, lo_sem, hi_sem, col_sent, left_sem, right_sem, piece_sent,
@@ -88,18 +89,29 @@
     face = lax.axis_index("face")
     sub = lax.axis_index("sub")
     me = face * 32 + sub
-    east = lax.rem(face + 1, 4)
-    west = lax.rem(face + 3, 4)
+    east = (face + 1) & 3
+    west = (face + 3) & 3
     first = sub == 0
     last = sub == 31
+    loads = [
+        pltpu.make_async_copy(source, target, load_sem.at[n])
+        for n, (source, target) in enumerate((
+            (field_hbm, field_ref), (dwk_hbm, dwk_ref), (dwb_hbm, dwb_ref), (zk_hbm, zk_ref),
+            (zb_hbm, zb_ref), (gain_hbm, gain_ref), (w_in_hbm, w_in_ref), (w_out_hbm, w_out_ref),
+            (ls_hbm, ls_ref)))
+    ]
+    loads[0].start()
     announce(face, sub)
+    for load in loads[1:]:
+        load.start()
+    loads[0].wait()
 
     def start(f, r, h=0):
         return (f * 12 + r * 2 + h) * PITCH + ROW
 
     def widen(t, carry):
-        f = t // 4
-        j = lax.rem(t, 4)
+        f = t >> 2
+        j = t & 3
         for h in range(2):
             grid[pl.ds(start(f, j + 1, h), SIDE), :] = field_ref[
                 f, j, :, h * LANES : (h + 1) * LANES
@@ -165,6 +177,9 @@
     pl.when(last)(lambda: scatter(west, right0, piece_sem.at[0]))
     pl.when(first)(lambda: scatter(east, left2, piece_sem.at[1]))
 
+    for load in loads[1:]:
+        load.wait()
+
     def weight(ref, tap, h):
         return ref[tap : tap + 1, h * LANES : (h + 1) * LANES]
 
@@ -261,16 +276,17 @@
 
     lax.fori_loop(0, 3, around, 0)
 
-    def pack(t, carry):
-        c = lax.rem(t + 4 * sub, ALL)
+    def pack(pf, ps):
+        c = pf * 32 + ps
+        t = (c - 4 * sub) & (ALL - 1)
         for f in range(3):
             cells = turned[pl.ds(f * FACE_ROWS + 8 + t, 8, stride=TURN), :]
             send[c, f] = cells.astype(jnp.bfloat16)
-        return carry
-
-    lax.fori_loop(0, ALL, pack, 0, unroll=8)
-    exchange(face, sub, me, send, recv, send_sem.at[0], recv_sem.at[0])
-    settle(face, sub, send, recv, send_sem.at[0], recv_sem.at[0])
+
+    exchange(face, sub, pack, send, recv, send_sem.at[3], recv_sem.at[3])
+    pack(face, sub)
+    recv[me] = send[me]
+    settle(face, sub, send, recv, send_sem.at[3], recv_sem.at[3])
     for cond, copy in inner:
         pl.when(cond)(copy.wait_send)
     pl.when(first | last)(
@@ -280,15 +296,15 @@
     row_in = lax.broadcasted_iota(jnp.int32, (8, LANES), 0) // 2
 
     def unpack(i, carry):
-        q = i // 32
-        s = lax.rem(i, 32)
+        q = i >> 5
+        s = i & 31
         at = (3 - q) * 32 + s
         upper = row_in + 4 * s > c
         north = recv[i, 0].astype(jnp.float32)
         middle = recv[i, 1].astype(jnp.float32)
         south = recv[i, 2].astype(jnp.float32)
         chain1[at + 3] = jnp.where(upper, middle, north)
-        before = recv[lax.rem(i + 96, ALL), 2].astype(jnp.float32)
+        before = recv[(i + 96) & (ALL - 1), 2].astype(jnp.float32)
         chain2[at + 3] = jnp.where(upper, before, middle)
         polar[pl.ds(pl.multiple_of(8 * i, 8), 8), :] = jnp.where(upper, north, south)
         return carry
@@ -298,6 +314,32 @@
         for e in range(3):
             chain[e] = chain[ALL + e]
             chain[ALL + 3 + e] = chain[3 + e]
+
+    def coeff(ref, k):
+        lo = jnp.broadcast_to(ref[k : k + 1, :LANES], (8, LANES))
+        hi = jnp.broadcast_to(ref[k : k + 1, LANES:], (8, LANES))
+        odd = lax.rem(lax.broadcasted_iota(jnp.int32, (8, LANES), 0), 2) == 1
+        return jnp.where(odd, hi, lo)
+
+    taps = [coeff(zk_ref, k) for k in range(TAPS)]
+    bias = coeff(zb_ref, 0)
+
+    def middle(pf, ps):
+        at = (3 - pf) * 32 + ps
+        i = pf * 32 + ps
+        upper = row_in + 4 * ps > c
+        z1 = bias
+        z2 = bias
+        for k in range(TAPS):
+            z1 = z1 + taps[k] * chain1[at + 6 - k]
+            z2 = z2 + taps[k] * chain2[at + 6 - k]
+        back_send[1, i] = jnp.where(upper, z1, z2).astype(jnp.bfloat16)
+        back_send[0, i] = z1.astype(jnp.bfloat16)
+        back_send[2, (i + 96) & (ALL - 1)] = z2.astype(jnp.bfloat16)
+
+    exchange(face, sub, middle, back_send.at[1], back_recv.at[1], send_sem.at[1], recv_sem.at[1])
+    middle(face, sub)
+    back_recv[1, me] = back_send[1, me]
 
     arc_n = SIDE - 1 - c
     arc_s = c + 1
@@ -314,15 +356,6 @@
         for e in range(1, 4):
             lin[pl.ds(base - 8 * e, 8), :] = lin[pl.ds(base - 8 * e + size, 8), :]
 
-    def coeff(ref, k):
-        lo = jnp.broadcast_to(ref[k : k + 1, :LANES], (8, LANES))
-        hi = jnp.broadcast_to(ref[k : k + 1, LANES:], (8, LANES))
-        odd = lax.rem(lax.broadcasted_iota(jnp.int32, (8, LANES), 0), 2) == 1
-        return jnp.where(odd, hi, lo)
-
-    taps = [coeff(zk_ref, k) for k in range(TAPS)]
-    bias = coeff(zb_ref, 0)
-
     def stencil_lin(v, carry):
         at = pl.multiple_of(BASE_N + 8 * v, 8)
         total = bias
@@ -338,37 +371,29 @@
         from_s = zlin[pl.ds(base_s + (3 - q) * 2 * arc_s, 256), :]
         polar[q * 256 : (q + 1) * 256, :] = jnp.where(row_256 > c, from_n, from_s)
 
-    def finish_zonal(i, carry):
-        q = i // 32
-        s = lax.rem(i, 32)
-        at = (3 - q) * 32 + s
-        upper = row_in + 4 * s > c
-        z1 = bias
-        z2 = bias
-        for k in range(TAPS):
-            z1 = z1 + taps[k] * chain1[at + 6 - k]
-            z2 = z2 + taps[k] * chain2[at + 6 - k]
-        zp = polar[pl.ds(pl.multiple_of(8 * i, 8), 8), :]
-        back_send[i, 0] = jnp.where(upper, zp, z1).astype(jnp.bfloat16)
-        back_send[i, 1] = jnp.where(upper, z1, z2).astype(jnp.bfloat16)
-        back = lax.rem(i + 96, ALL)
-        zp = polar[pl.ds(pl.multiple_of(8 * back, 8), 8), :]
-        back_send[back, 2] = jnp.where(upper, z2, zp).astype(jnp.bfloat16)
-        return carry
-
-    lax.fori_loop(0, ALL, finish_zonal, 0, unroll=2)
-    exchange(face, sub, me, back_send, back_recv, send_sem.at[1], recv_sem.at[1])
-    settle(face, sub, back_send, back_recv, send_sem.at[1], recv_sem.at[1])
-
-    def unturn(i, carry):
-        t = lax.rem(i + ALL - 4 * sub, ALL)
-        for f in range(3):
-            turned[pl.ds(f * FACE_ROWS + 8 + t, 8, stride=TURN), :] = back_recv[i, f].astype(
+    def ends(f):
+        def one(pf, ps):
+            i = pf * 32 + ps
+            upper = row_in + 4 * ps > c
+            zp = polar[pl.ds(pl.multiple_of(8 * i, 8), 8), :]
+            zm = back_send[f, i].astype(jnp.float32)
+            back_send[f, i] = jnp.where(upper == (f == 0), zp, zm).astype(jnp.bfloat16)
+
+        exchange(face, sub, one, back_send.at[f], back_recv.at[f], send_sem.at[f], recv_sem.at[f])
+        one(face, sub)
+        back_recv[f, me] = back_send[f, me]
+
+    ends(0)
+    ends(2)
+
+    def unturn(f):
+        def one(i, carry):
+            t = (i - 4 * sub) & (ALL - 1)
+            turned[pl.ds(f * FACE_ROWS + 8 + t, 8, stride=TURN), :] = back_recv[f, i].astype(
                 jnp.float32)
-        return carry
-
-    lax.fori_loop(0, ALL, unturn, 0, unroll=8)
-    for f in range(3):
+            return carry
+
+        lax.fori_loop(0, ALL, one, 0, unroll=8)
         for j in range(1, 4):
             for h in range(2):
                 turned[pl.ds(slot(f, j, h) + SIDE - j, j), :] = turned[
@@ -379,9 +404,7 @@
     w_in = w_in_ref[...]
     w_out = w_out_ref[...]
 
-    def mlp(t, carry):
-        f = t // 4
-        j = lax.rem(t, 4)
+    def mlp(f, j, carry):
         base = f * FACE_ROWS + 2 * j * TURN + j + 8
         values = jnp.concatenate(
             [turned[pl.ds(base, SIDE), :], turned[pl.ds(base + TURN, SIDE), :]], axis=1
@@ -397,7 +420,10 @@
         out_ref[f, j] = result.astype(jnp.bfloat16)
         return carry
 
-    lax.fori_loop(0, 12, mlp, 0)
+    for f in (1, 0, 2):
+        settle(face, sub, back_send.at[f], back_recv.at[f], send_sem.at[f], recv_sem.at[f])
+        unturn(f)
+        lax.fori_loop(0, 4, functools.partial(mlp, f), 0)
 
 
 def run(field, dw_kernel, dw_bias, zonal_kernel, zonal_bias, norm_gain, w_in, w_out, layer_scale):
@@ -406,13 +432,25 @@
     lines = pltpu.VMEM((3, SIDE, 2 * LANES), jnp.bfloat16)
     tiles = lambda *lead: pltpu.VMEM((*lead, 8, LANES), jnp.bfloat16)
     rows = lambda n: pltpu.VMEM((n, LANES), jnp.float32)
+    vector = pltpu.VMEM((1, 2 * LANES), jnp.float32)
+    back = pltpu.VMEM((3, ALL, 8, LANES), jnp.bfloat16)
     dma = pltpu.SemaphoreType.DMA
     return pl.pallas_call(
         kernel,
         out_shape=jax.ShapeDtypeStruct(field.shape, jnp.bfloat16),
-        in_specs=[vmem] * 9,
+        in_specs=[pl.BlockSpec(memory_space=pltpu.HBM)] * 9,
         out_specs=vmem,
         scratch_shapes=[
+            pltpu.VMEM(field.shape, field.dtype),
+            pltpu.VMEM(dw_kernel.shape, jnp.float32),
+            vector,
+            pltpu.VMEM(zonal_kernel.shape, jnp.float32),
+            vector,
+            vector,
+            pltpu.VMEM(w_in.shape, w_in.dtype),
+            pltpu.VMEM(w_out.shape, w_out.dtype),
+            vector,
+            dma((9,)),
             rows(36 * PITCH + 16),
             lines,
             lines,
@@ -433,10 +471,10 @@
             rows(1024),
             rows(LIN_ROWS),
             rows(LIN_ROWS),
-            cells,
-            cells,
-            dma((2,)),
-            dma((2,)),
+            back,
+            back,
+            dma((4,)),
+            dma((4,)),
             dma((2, 3)),
             dma((3,)),
             dma((3,)),
@@ -449,12 +487,12 @@
             dma((2,)),
         ],
         compiler_params=pltpu.CompilerParams(
-            collective_id=0, has_side_effects=True, vmem_limit_bytes=56 * 1024 * 1024
+            collective_id=0, has_side_effects=True, vmem_limit_bytes=24 * 1024 * 1024
         ),
-    )(
+    )(*[pltpu.with_memory_space_constraint(a, pltpu.HBM) for a in (
         field, dw_kernel, dw_bias[None], zonal_kernel, zonal_bias[None], norm_gain[None], w_in,
         w_out, layer_scale[None],
-    )
+    )])
 
 
 def shards(

time: 60.7 us -> 47.4 us (0.78)
  Pallas kernels: 58.4 us -> 46.4 us
  local copies, waits for them, and re-layouts: 2.06 us -> 0.88 us
    pallas_call x1, Pallas kernels: 58.4 us -> 46.4 us  [run(): pl.pallas_call(kernel, out_shape=jax.ShapeDtypeStruct(field.shape, jnp.bf...]
    unnamed x1, local copies, waits for them, and re-layouts: 2.06 us -> 0.88 us
where the time goes in v3:
time: 47.4 us; the launch traced here: 47.3 us
  Pallas kernels  46.4 us (98%)
  local copies, waits for them, and re-layouts  0.88 us (2%)
    pallas_call x1, Pallas kernels, run(): pl.pallas_call(kernel, out_shape=jax.ShapeDtypeStruct(field.shape, jnp.bf...  46.4 us

profile of v3, /device:TPU:1, one launch (start us, length us, event | category | flops | bytes accessed | tf_op | source)
XLA Modules:
  0.0 47.3 jit_solution(9234002584035023243)
XLA Ops:
  0.0 46.4 %shard_map.91 = bf16[3,4,128,256]{3,2,1,0:T(8,128)(2,1)S(1)} custom-call(bf16[3,4,128,256]{3,2,1,0:T(8,128)(2,1)} %bitcast.9, f32[9,256]{1,0:T(8,128)} %dwk_hbm.1, f32[1,256]{1,0:T(1,128)} %bitcast.10, f32[7,256]{1,0:T(8,128)} %zk_hbm.1, f32[1,256]{1,0:T(1,128)} %bitcast.11, f32[1,256]{1,0:T(1,128)} %bitcast.12, bf16[256,768]{1,0:T(8,128)(2,1)} %w_in_hbm.1, ...), custom_call_target="tpu_custom_call" | custom-call | tf_op jit(solution)/shard_map/pallas_call | solution.py:438
  46.4 0.9 %copy.12 = bf16[3,1,4,128,256]{4,3,2,1,0:T(8,128)(2,1)} copy(bf16[3,1,4,128,256]{4,3,2,1,0:T(8,128)(2,1)S(1)} %bitcast.8) | data formatting | bytes 1572864

commit v4 on v3

--- a/solution.py
+++ b/solution.py
@@ -19,7 +19,7 @@
 FACE_ROWS = 8 * TURN + 16
 BASE_N = 288
 LIN_ROWS = 1664
-ZROWS = 1072
+LIN_BLOCKS = 17
 
 
 def peer_at(face, sub, step):
@@ -65,8 +65,26 @@
     push(*lax.fori_loop(2, ALL, step, (pf, ps), unroll=2))
 
 
-def settle(face, sub, source, target, send_sem, recv_sem):
-    whole = pltpu.make_async_remote_copy(
+def dispatch(face, sub, source, target, send_sem, recv_sem):
+    me = face * 32 + sub
+
+    def step(i, carry):
+        pf, ps = peer_at(face, sub, ALL - i)
+        pltpu.make_async_remote_copy(
+            source.at[pf * 32 + ps],
+            target.at[me],
+            send_sem,
+            recv_sem,
+            device_id=(pf, ps),
+            device_id_type=MESH,
+        ).start()
+        return carry
+
+    lax.fori_loop(1, ALL, step, 0, unroll=2)
+
+
+def all_blocks(face, sub, source, target, send_sem, recv_sem):
+    return pltpu.make_async_remote_copy(
         source.at[pl.ds(0, ALL - 1)],
         target.at[pl.ds(0, ALL - 1)],
         send_sem,
@@ -74,15 +92,13 @@
         device_id=(face, sub),
         device_id_type=MESH,
     )
-    whole.wait_send()
-    whole.wait_recv()
 
 
 def kernel(
     field_hbm, dwk_hbm, dwb_hbm, zk_hbm, zb_hbm, gain_hbm, w_in_hbm, w_out_hbm, ls_hbm, out_ref,
     field_ref, dwk_ref, dwb_ref, zk_ref, zb_ref, gain_ref, w_in_ref, w_out_ref, ls_ref, load_sem,
     grid, row_lo, row_hi, cols, left1, right2, pieces, right0, left2, rim_hi, rim_lo, rim_rows,
-    turned, send, recv, chain1, chain2, polar, lin, zlin, back_send, back_recv,
+    turned, send, recv, chain, ring, polar, lin, zlin, back_send, back_recv,
     send_sem, recv_sem, row_sent, lo_sem, hi_sem, col_sent, left_sem, right_sem, piece_sent,
     piece_sem, rim_sent, rim_sem,
 ):
@@ -276,45 +292,23 @@
 
     lax.fori_loop(0, 3, around, 0)
 
-    def pack(pf, ps):
-        c = pf * 32 + ps
-        t = (c - 4 * sub) & (ALL - 1)
-        for f in range(3):
-            cells = turned[pl.ds(f * FACE_ROWS + 8 + t, 8, stride=TURN), :]
-            send[c, f] = cells.astype(jnp.bfloat16)
-
-    exchange(face, sub, pack, send, recv, send_sem.at[3], recv_sem.at[3])
-    pack(face, sub)
-    recv[me] = send[me]
-    settle(face, sub, send, recv, send_sem.at[3], recv_sem.at[3])
-    for cond, copy in inner:
-        pl.when(cond)(copy.wait_send)
-    pl.when(first | last)(
-        lambda: push(pieces, pieces, piece_sent, piece_sem.at[0], face, sub).wait_send())
+    high = (0, 1, 2)
+    low = (2, 0, 1)
+    row_in = lax.broadcasted_iota(jnp.int32, (8, LANES), 0) // 2
+    for g in range(3):
+
+        def pack(pf, ps, g=g):
+            c = pf * 32 + ps
+            t = (c - 4 * sub) & (ALL - 1)
+            above = turned[pl.ds(high[g] * FACE_ROWS + 8 + t, 8, stride=TURN), :]
+            below = turned[pl.ds(low[g] * FACE_ROWS + 8 + t, 8, stride=TURN), :]
+            send[g, c] = jnp.where(row_in + 4 * sub > c, above, below).astype(jnp.bfloat16)
+
+        exchange(face, sub, pack, send.at[g], recv.at[g], send_sem.at[g], recv_sem.at[g])
+        pack(face, sub)
+        recv[g, me] = send[g, me]
 
     c = me
-    row_in = lax.broadcasted_iota(jnp.int32, (8, LANES), 0) // 2
-
-    def unpack(i, carry):
-        q = i >> 5
-        s = i & 31
-        at = (3 - q) * 32 + s
-        upper = row_in + 4 * s > c
-        north = recv[i, 0].astype(jnp.float32)
-        middle = recv[i, 1].astype(jnp.float32)
-        south = recv[i, 2].astype(jnp.float32)
-        chain1[at + 3] = jnp.where(upper, middle, north)
-        before = recv[(i + 96) & (ALL - 1), 2].astype(jnp.float32)
-        chain2[at + 3] = jnp.where(upper, before, middle)
-        polar[pl.ds(pl.multiple_of(8 * i, 8), 8), :] = jnp.where(upper, north, south)
-        return carry
-
-    lax.fori_loop(0, ALL, unpack, 0, unroll=4)
-    for chain in (chain1, chain2):
-        for e in range(3):
-            chain[e] = chain[ALL + e]
-            chain[ALL + 3 + e] = chain[3 + e]
-
     def coeff(ref, k):
         lo = jnp.broadcast_to(ref[k : k + 1, :LANES], (8, LANES))
         hi = jnp.broadcast_to(ref[k : k + 1, LANES:], (8, LANES))
@@ -324,23 +318,27 @@
     taps = [coeff(zk_ref, k) for k in range(TAPS)]
     bias = coeff(zb_ref, 0)
 
-    def middle(pf, ps):
-        at = (3 - pf) * 32 + ps
-        i = pf * 32 + ps
-        upper = row_in + 4 * ps > c
-        z1 = bias
-        z2 = bias
-        for k in range(TAPS):
-            z1 = z1 + taps[k] * chain1[at + 6 - k]
-            z2 = z2 + taps[k] * chain2[at + 6 - k]
-        back_send[1, i] = jnp.where(upper, z1, z2).astype(jnp.bfloat16)
-        back_send[0, i] = z1.astype(jnp.bfloat16)
-        back_send[2, (i + 96) & (ALL - 1)] = z2.astype(jnp.bfloat16)
-
-    exchange(face, sub, middle, back_send.at[1], back_recv.at[1], send_sem.at[1], recv_sem.at[1])
-    middle(face, sub)
-    back_recv[1, me] = back_send[1, me]
-
+    def blend(terms):
+        products = [tap * term for tap, term in zip(taps, terms)]
+        return ((products[0] + products[1]) + (products[2] + products[3])) + (
+            (products[4] + products[5]) + (products[6] + bias))
+
+    def arrive(g):
+        all_blocks(face, sub, send.at[g], recv.at[g], send_sem.at[g], recv_sem.at[g]).wait_recv()
+
+    def depart(g):
+        back_recv[g, me] = back_send[g, me]
+        dispatch(
+            face, sub, back_send.at[g], back_recv.at[g], send_sem.at[3 + g], recv_sem.at[3 + g])
+
+    arrive(0)
+
+    def lay(b, carry):
+        rows = recv[0, pl.ds(8 * b, 8)].astype(jnp.float32)
+        polar[pl.ds(pl.multiple_of(64 * b, 64), 64), :] = rows.reshape(64, LANES)
+        return carry
+
+    lax.fori_loop(0, 16, lay, 0, unroll=2)
     arc_n = SIDE - 1 - c
     arc_s = c + 1
     base_s = BASE_N + 8 * arc_n + 48
@@ -356,56 +354,77 @@
         for e in range(1, 4):
             lin[pl.ds(base - 8 * e, 8), :] = lin[pl.ds(base - 8 * e + size, 8), :]
 
+
     def stencil_lin(v, carry):
-        at = pl.multiple_of(BASE_N + 8 * v, 8)
-        total = bias
-        for k in range(TAPS):
-            total = total + taps[k] * lin[pl.ds(pl.multiple_of(at - 8 * (k - 3), 8), 8), :]
-        zlin[pl.ds(at, 8), :] = total
-        return carry
-
-    lax.fori_loop(0, ZROWS // 8, stencil_lin, 0, unroll=2)
+        at = pl.multiple_of(BASE_N + 64 * v, 8)
+        window = [lin[pl.ds(pl.multiple_of(at + 8 * (n - 3), 8), 8), :] for n in range(14)]
+        for n in range(8):
+            zlin[pl.ds(pl.multiple_of(at + 8 * n, 8), 8), :] = blend(window[n : n + 7][::-1])
+        return carry
+
+    lax.fori_loop(0, LIN_BLOCKS, stencil_lin, 0)
     row_256 = lax.broadcasted_iota(jnp.int32, (256, LANES), 0) // 2
     for q in range(4):
         from_n = zlin[pl.ds(BASE_N + (3 - q) * 2 * arc_n - 2 * (c + 1), 256), :]
         from_s = zlin[pl.ds(base_s + (3 - q) * 2 * arc_s, 256), :]
-        polar[q * 256 : (q + 1) * 256, :] = jnp.where(row_256 > c, from_n, from_s)
-
-    def ends(f):
-        def one(pf, ps):
-            i = pf * 32 + ps
-            upper = row_in + 4 * ps > c
-            zp = polar[pl.ds(pl.multiple_of(8 * i, 8), 8), :]
-            zm = back_send[f, i].astype(jnp.float32)
-            back_send[f, i] = jnp.where(upper == (f == 0), zp, zm).astype(jnp.bfloat16)
-
-        exchange(face, sub, one, back_send.at[f], back_recv.at[f], send_sem.at[f], recv_sem.at[f])
-        one(face, sub)
-        back_recv[f, me] = back_send[f, me]
-
-    ends(0)
-    ends(2)
-
-    def unturn(f):
-        def one(i, carry):
-            t = (i - 4 * sub) & (ALL - 1)
-            turned[pl.ds(f * FACE_ROWS + 8 + t, 8, stride=TURN), :] = back_recv[f, i].astype(
-                jnp.float32)
+        back_send[0, pl.ds(32 * q, 32)] = (
+            jnp.where(row_256 > c, from_n, from_s).reshape(32, 8, LANES).astype(jnp.bfloat16))
+    depart(0)
+
+    block_row = 4 * lax.broadcasted_iota(jnp.int32, (8, 8, LANES), 0) + (
+        lax.broadcasted_iota(jnp.int32, (8, 8, LANES), 1) // 2)
+
+    for g in (1, 2):
+        arrive(g)
+
+        def unpack(b, carry, g=g):
+            at = pl.multiple_of(8 * b, 8)
+            i = (3 - (b >> 2)) * 32 + 8 * (b & 3)
+            rows = recv[g, pl.ds(i, 8)].astype(jnp.float32)
+            if g == 2:
+                before = recv[g, pl.ds((i + 96) & (ALL - 1), 8)].astype(jnp.float32)
+                rows = jnp.where(block_row + 32 * (b & 3) > c, before, rows)
+            chain[pl.ds(at + 3, 8)] = rows
             return carry
 
-        lax.fori_loop(0, ALL, one, 0, unroll=8)
-        for j in range(1, 4):
-            for h in range(2):
-                turned[pl.ds(slot(f, j, h) + SIDE - j, j), :] = turned[
-                    pl.ds(slot(f, j, h) - j, j), :]
+        lax.fori_loop(0, 16, unpack, 0, unroll=2)
+        for e in range(3):
+            chain[e] = chain[ALL + e]
+            chain[ALL + 3 + e] = chain[3 + e]
+
+        def stencil_ring(b, carry, g=g):
+            at = 8 * b
+            i = (3 - (b >> 2)) * 32 + 8 * (b & 3)
+            window = [chain[at + n] for n in range(14)]
+            for n in range(8):
+                total = blend(window[n : n + 7][::-1])
+                if g == 1:
+                    back_send[g, i + n] = total.astype(jnp.bfloat16)
+                else:
+                    ring[i + n] = total
+            return carry
+
+        lax.fori_loop(0, 16, stencil_ring, 0)
+        if g == 2:
+
+            def regroup(b, carry):
+                rows = ring[pl.ds(8 * b, 8)]
+                after = ring[pl.ds((8 * b + 32) & (ALL - 1), 8)]
+                back_send[2, pl.ds(8 * b, 8)] = jnp.where(
+                    block_row + 32 * (b & 3) > c, after, rows).astype(jnp.bfloat16)
+                return carry
+
+            lax.fori_loop(0, 16, regroup, 0, unroll=2)
+        depart(g)
 
     gain = gain_ref[...]
     scale = ls_ref[...]
     w_in = w_in_ref[...]
     w_out = w_out_ref[...]
-
-    def mlp(f, j, carry):
-        base = f * FACE_ROWS + 2 * j * TURN + j + 8
+    column = lax.broadcasted_iota(jnp.int32, (SIDE, 2 * LANES), 0)
+
+    def mlp(g, j, carry):
+        base = g * FACE_ROWS + 2 * j * TURN + j + 8
         values = jnp.concatenate(
             [turned[pl.ds(base, SIDE), :], turned[pl.ds(base + TURN, SIDE), :]], axis=1
         )
@@ -416,24 +435,52 @@
         pre = jnp.dot(normed, w_in, preferred_element_type=jnp.float32)
         hidden = (0.5 * pre * (1.0 + lax.erf(pre * np.float32(np.sqrt(0.5))))).astype(jnp.bfloat16)
         branch = jnp.dot(hidden, w_out, preferred_element_type=jnp.float32)
-        result = field_ref[f, j].astype(jnp.float32) + scale * branch
-        out_ref[f, j] = result.astype(jnp.bfloat16)
-        return carry
-
-    for f in (1, 0, 2):
-        settle(face, sub, back_send.at[f], back_recv.at[f], send_sem.at[f], recv_sem.at[f])
-        unturn(f)
-        lax.fori_loop(0, 4, functools.partial(mlp, f), 0)
+        upper = column + 4 * sub + j >= SIDE
+        source = jnp.where(
+            upper, field_ref[high[g], j].astype(jnp.float32), field_ref[low[g], j].astype(jnp.float32))
+        result = source + scale * branch
+        for f, kept in ((high[g], upper), (low[g], jnp.logical_not(upper))):
+            seen = (g, f) in ((1, 0), (2, 1), (2, 2))
+            row = jnp.where(kept, result, out_ref[f, j].astype(jnp.float32)) if seen else result
+            out_ref[f, j] = row.astype(jnp.bfloat16)
+        return carry
+
+    for g in range(3):
+        all_blocks(
+            face, sub, back_send.at[g], back_recv.at[g], send_sem.at[3 + g], recv_sem.at[3 + g]
+        ).wait_recv()
+
+        def unturn(i, carry, g=g):
+            t = (i - 4 * sub) & (ALL - 1)
+            turned[pl.ds(g * FACE_ROWS + 8 + t, 8, stride=TURN), :] = back_recv[g, i].astype(
+                jnp.float32)
+            return carry
+
+        lax.fori_loop(0, ALL, unturn, 0, unroll=8)
+        for j in range(1, 4):
+            for h in range(2):
+                turned[pl.ds(slot(g, j, h) + SIDE - j, j), :] = turned[
+                    pl.ds(slot(g, j, h) - j, j), :]
+        lax.fori_loop(0, 4, functools.partial(mlp, g), 0)
+
+    for cond, copy in inner:
+        pl.when(cond)(copy.wait_send)
+    pl.when(first | last)(
+        lambda: push(pieces, pieces, piece_sent, piece_sem.at[0], face, sub).wait_send())
+    for g in range(3):
+        all_blocks(face, sub, send.at[g], recv.at[g], send_sem.at[g], recv_sem.at[g]).wait_send()
+        all_blocks(
+            face, sub, back_send.at[g], back_recv.at[g], send_sem.at[3 + g], recv_sem.at[3 + g]
+        ).wait_send()
 
 
 def run(field, dw_kernel, dw_bias, zonal_kernel, zonal_bias, norm_gain, w_in, w_out, layer_scale):
     vmem = pl.BlockSpec(memory_space=pltpu.VMEM)
-    cells = pltpu.VMEM((ALL, 3, 8, LANES), jnp.bfloat16)
     lines = pltpu.VMEM((3, SIDE, 2 * LANES), jnp.bfloat16)
     tiles = lambda *lead: pltpu.VMEM((*lead, 8, LANES), jnp.bfloat16)
     rows = lambda n: pltpu.VMEM((n, LANES), jnp.float32)
     vector = pltpu.VMEM((1, 2 * LANES), jnp.float32)
-    back = pltpu.VMEM((3, ALL, 8, LANES), jnp.bfloat16)
+    blocks = pltpu.VMEM((3, ALL, 8, LANES), jnp.bfloat16)
     dma = pltpu.SemaphoreType.DMA
     return pl.pallas_call(
         kernel,
@@ -464,17 +511,17 @@
             tiles(32),
             rows(2 * SIDE),
             rows(3 * FACE_ROWS + 8),
-            cells,
-            cells,
+            blocks,
+            blocks,
             pltpu.VMEM((ALL + 6, 8, LANES), jnp.float32),
-            pltpu.VMEM((ALL + 6, 8, LANES), jnp.float32),
+            pltpu.VMEM((ALL, 8, LANES), jnp.float32),
             rows(1024),
             rows(LIN_ROWS),
             rows(LIN_ROWS),
-            back,
-            back,
-            dma((4,)),
-            dma((4,)),
+            blocks,
+            blocks,
+            dma((6,)),
+            dma((6,)),
             dma((2, 3)),
             dma((3,)),
             dma((3,)),

time: 47.4 us -> 43.3 us (0.914)
  Pallas kernels: 46.4 us -> 42.4 us
    pallas_call x1, Pallas kernels: 46.4 us -> 42.4 us  [run(): pl.pallas_call(kernel, out_shape=jax.ShapeDtypeStruct(field.shape, jnp.bf...]
where the time goes in v4:
time: 43.3 us; the launch traced here: 43.2 us
  Pallas kernels  42.4 us (98%)
  local copies, waits for them, and re-layouts  0.88 us (2%)
    pallas_call x1, Pallas kernels, run(): pl.pallas_call(kernel, out_shape=jax.ShapeDtypeStruct(field.shape, jnp.bf...  42.4 us
    unnamed x1, local copies, waits for them, and re-layouts  0.88 us

profile of v4, /device:TPU:1, one launch (start us, length us, event | category | flops | bytes accessed | tf_op | source)
XLA Modules:
  0.0 43.2 jit_solution(8690487937349586291)
XLA Ops:
  0.0 42.4 %shard_map.91 = bf16[3,4,128,256]{3,2,1,0:T(8,128)(2,1)S(1)} custom-call(bf16[3,4,128,256]{3,2,1,0:T(8,128)(2,1)} %bitcast.9, f32[9,256]{1,0:T(8,128)} %dwk_hbm.1, f32[1,256]{1,0:T(1,128)} %bitcast.10, f32[7,256]{1,0:T(8,128)} %zk_hbm.1, f32[1,256]{1,0:T(1,128)} %bitcast.11, f32[1,256]{1,0:T(1,128)} %bitcast.12, bf16[256,768]{1,0:T(8,128)(2,1)} %w_in_hbm.1, ...), custom_call_target="tpu_custom_call" | custom-call | tf_op jit(solution)/shard_map/pallas_call | solution.py:485
  42.4 0.9 %copy.12 = bf16[3,1,4,128,256]{4,3,2,1,0:T(8,128)(2,1)} copy(bf16[3,1,4,128,256]{4,3,2,1,0:T(8,128)(2,1)S(1)} %bitcast.8) | data formatting | bytes 1572864

commit v5 on v4

--- a/solution.py
+++ b/solution.py
@@ -30,29 +30,53 @@
     return pf, (px << 3) + (pz << 1) + pc
 
 
+def greet(sem, pf, ps):
+    pl.semaphore_signal(sem, inc=1, device_id=(pf, ps), device_id_type=MESH)
+
+
 def announce(face, sub):
     barrier = pltpu.get_barrier_semaphore()
-
-    def greet(i, carry):
-        pf, ps = peer_at(face, sub, ALL - i)
-        pl.semaphore_signal(barrier, inc=1, device_id=(pf, ps), device_id_type=MESH)
-        return carry
-
-    lax.fori_loop(1, ALL, greet, 0, unroll=2)
-
-
-def exchange(face, sub, prepare, source, target, send_sem, recv_sem):
+    east = (face + 1) & 3
+    west = (face + 3) & 3
+    for n in range(1, 8):
+        greet(barrier, face, (sub & 24) + ((sub + n) & 7))
+    for n in range(1, 4):
+        greet(barrier, face, (sub + 8 * n) & 31)
+        greet(barrier, (face + n) & 3, sub)
+    edge = sub & 7
+    for cond, pf, ps in (
+        (sub > 0, east, sub - 1),
+        (sub > 0, west, sub - 1),
+        (sub < 31, east, sub + 1),
+        (sub < 31, west, sub + 1),
+        ((edge == 7) & (sub < 31), face, sub + 1),
+        ((edge == 0) & (sub > 0), face, sub - 1),
+        (sub == 31, face, 0),
+        (sub == 31, west, 0),
+        (sub == 0, face, 31),
+        (sub == 0, east, 31),
+    ):
+        pl.when(cond)(functools.partial(greet, barrier, pf, ps))
+    inner_edge = ((edge == 0) | (edge == 7)) & (sub > 0) & (sub < 31)
+    return 17 + inner_edge.astype(jnp.int32)
+
+
+def exchange(face, sub, prepare, source, target, send_sem, recv_sem, later=None):
     me = face * 32 + sub
 
     def push(pf, ps):
-        pltpu.make_async_remote_copy(
+        copy = pltpu.make_async_remote_copy(
             source.at[pf * 32 + ps],
             target.at[me],
             send_sem,
             recv_sem,
             device_id=(pf, ps),
             device_id_type=MESH,
-        ).start()
+        )
+        if later is None:
+            copy.start()
+        else:
+            pl.when(pf * 32 + ps != later)(copy.start)
 
     def step(i, carry):
         pf, ps = peer_at(face, sub, ALL - i)
@@ -99,7 +123,7 @@
     field_ref, dwk_ref, dwb_ref, zk_ref, zb_ref, gain_ref, w_in_ref, w_out_ref, ls_ref, load_sem,
     grid, row_lo, row_hi, cols, left1, right2, pieces, right0, left2, rim_hi, rim_lo, rim_rows,
     turned, send, recv, chain, ring, polar, lin, zlin, back_send, back_recv,
-    send_sem, recv_sem, row_sent, lo_sem, hi_sem, col_sent, left_sem, right_sem, piece_sent,
+    send_sem, recv_sem, round_sem, row_sent, lo_sem, hi_sem, col_sent, left_sem, right_sem, piece_sent,
     piece_sem, rim_sent, rim_sem,
 ):
     face = lax.axis_index("face")
@@ -117,7 +141,7 @@
             (ls_hbm, ls_ref)))
     ]
     loads[0].start()
-    announce(face, sub)
+    partners = announce(face, sub)
     for load in loads[1:]:
         load.start()
     loads[0].wait()
@@ -174,24 +198,17 @@
             cols.at[0], left1.at[1 - d], col_sent.at[0, 1 - d], left_sem.at[1 - d], east, sub + d)))
         inner.append((cond, push(
             cols.at[1], right2.at[1 - d], col_sent.at[1, 1 - d], right_sem.at[1 - d], west, sub + d)))
-    inner.append((sub >= 0, push(
-        cols.at[2], rim_hi.at[sub], rim_sent.at[0], rim_sem.at[0], east, 31)))
-    inner.append((sub >= 0, push(
-        cols.at[3], rim_lo.at[sub], rim_sent.at[1], rim_sem.at[1], west, 0)))
-
-    pl.semaphore_wait(pltpu.get_barrier_semaphore(), ALL - 1)
+    outer = []
+    outer.append(push(
+        cols.at[2], rim_hi.at[sub], rim_sent.at[0], rim_sem.at[0], east, 31))
+    outer.append(push(
+        cols.at[3], rim_lo.at[sub], rim_sent.at[1], rim_sem.at[1], west, 0))
+
+    pl.semaphore_wait(pltpu.get_barrier_semaphore(), partners)
     for cond, copy in inner:
         pl.when(cond)(copy.start)
-
-    def scatter(pf, target, got):
-        def one(t, carry):
-            push(pieces.at[t], target, piece_sent, got, pf, t).start()
-            return carry
-
-        lax.fori_loop(0, 32, one, 0)
-
-    pl.when(last)(lambda: scatter(west, right0, piece_sem.at[0]))
-    pl.when(first)(lambda: scatter(east, left2, piece_sem.at[1]))
+    for n in range(1, 4):
+        greet(round_sem.at[0], face, (sub + 8 * n) & 31)
 
     for load in loads[1:]:
         load.wait()
@@ -219,7 +236,24 @@
                         zero, f, j, h, x, 56, rows)
         return carry
 
-    lax.fori_loop(0, 3, inside, 0)
+    inside(0, 0)
+    pl.semaphore_wait(round_sem.at[0], 3)
+    for n in range(1, 4):
+        greet(round_sem.at[1], (face + n) & 3, sub)
+    lax.fori_loop(1, 3, inside, 0)
+    pl.semaphore_wait(round_sem.at[1], 3)
+    for copy in outer:
+        copy.start()
+
+    def scatter(pf, target, got):
+        def one(t, carry):
+            push(pieces.at[t], target, piece_sent, got, pf, t).start()
+            return carry
+
+        lax.fori_loop(0, 32, one, 0)
+
+    pl.when(last)(lambda: scatter(west, right0, piece_sem.at[0]))
+    pl.when(first)(lambda: scatter(east, left2, piece_sem.at[1]))
 
     def took(ref, sem):
         push(ref, ref, row_sent.at[0, 0], sem, face, sub).wait_recv()
@@ -229,8 +263,6 @@
             lambda f=f: took(row_lo.at[f], lo_sem.at[f]))
         pl.when((sub < 31) if f == 0 else (sub >= 0))(
             lambda f=f: took(row_hi.at[f], hi_sem.at[f]))
-    took(right0, piece_sem.at[0])
-    took(left2, piece_sem.at[1])
     for e, cond in ((0, sub > 0), (1, sub >= 0), (2, sub < 31)):
         pl.when(cond)(lambda e=e: took(left1.at[e], left_sem.at[e]))
         pl.when(cond)(lambda e=e: took(right2.at[e], right_sem.at[e]))
@@ -240,15 +272,6 @@
             half = slice(h * LANES, (h + 1) * LANES)
             grid[pl.ds(start(f, 0, h), SIDE), :] = row_lo[f, :, half].astype(jnp.float32)
             grid[pl.ds(start(f, 5, h), SIDE), :] = row_hi[f, :, half].astype(jnp.float32)
-
-    def rim(ref, sem, f, r):
-        took(ref, sem)
-        rim_rows[...] = ref[...].astype(jnp.float32).reshape(2 * SIDE, LANES)
-        for h in range(2):
-            grid[pl.ds(start(f, r, h), SIDE), :] = rim_rows[pl.ds(h, SIDE, stride=2), :]
-
-    pl.when(first)(lambda: rim(rim_lo, rim_sem.at[1], 2, 0))
-    pl.when(last)(lambda: rim(rim_hi, rim_sem.at[0], 0, 5))
 
     for r, size in ((0, 8), (4, 4)):
         grid[pl.ds(start(0, r) - 1, size, stride=PITCH), :] = grid[
@@ -261,10 +284,6 @@
         grid[pl.ds(start(f, 0) + x, 2, stride=PITCH), :] = before[6:8]
         grid[pl.ds(start(f, 1) + x, 8, stride=PITCH), :] = ref[1].astype(jnp.float32)
         grid[pl.ds(start(f, 5) + x, 2, stride=PITCH), :] = after[0:2]
-    for f, x, ref in ((0, SIDE, right0), (2, -1, left2)):
-        for h in range(2):
-            grid[pl.ds(start(f, 0, h) + x, 6, stride=2 * PITCH), :] = ref[h].astype(jnp.float32)[:6]
-
     def corners(r):
         for f in range(3):
             for x in (-1, SIDE):
@@ -295,18 +314,68 @@
     high = (0, 1, 2)
     low = (2, 0, 1)
     row_in = lax.broadcasted_iota(jnp.int32, (8, LANES), 0) // 2
-    for g in range(3):
-
-        def pack(pf, ps, g=g):
+
+    def send_family(g, later=None):
+        def pack(pf, ps):
             c = pf * 32 + ps
             t = (c - 4 * sub) & (ALL - 1)
             above = turned[pl.ds(high[g] * FACE_ROWS + 8 + t, 8, stride=TURN), :]
             below = turned[pl.ds(low[g] * FACE_ROWS + 8 + t, 8, stride=TURN), :]
             send[g, c] = jnp.where(row_in + 4 * sub > c, above, below).astype(jnp.bfloat16)
 
-        exchange(face, sub, pack, send.at[g], recv.at[g], send_sem.at[g], recv_sem.at[g])
+        exchange(
+            face, sub, pack, send.at[g], recv.at[g], send_sem.at[g], recv_sem.at[g], later)
         pack(face, sub)
         recv[g, me] = send[g, me]
+        return pack
+
+    send_family(2)
+    pack_1 = send_family(1, ALL - 1)
+
+    def rim(ref, sem, f, r):
+        took(ref, sem)
+        rim_rows[...] = ref[...].astype(jnp.float32).reshape(2 * SIDE, LANES)
+        for h in range(2):
+            grid[pl.ds(start(f, r, h), SIDE), :] = rim_rows[pl.ds(h, SIDE, stride=2), :]
+
+    pl.when(first)(lambda: rim(rim_lo, rim_sem.at[1], 2, 0))
+    pl.when(last)(lambda: rim(rim_hi, rim_sem.at[0], 0, 5))
+
+    took(right0, piece_sem.at[0])
+    took(left2, piece_sem.at[1])
+    for f, x, ref in ((0, SIDE, right0), (2, -1, left2)):
+        for h in range(2):
+            grid[pl.ds(start(f, 0, h) + x, 6, stride=2 * PITCH), :] = ref[h].astype(jnp.float32)[:6]
+
+    pl.when(first)(lambda: corners(0))
+    pl.when(last)(lambda: corners(5))
+
+    def redo(f, j, h, x, size):
+        total = jnp.broadcast_to(weight(dwb_ref, 0, h), (size, LANES))
+        turned[pl.ds(slot(f, j, h) + x, size), :] = partial_sum(
+            total, f, j, h, x, size, (0, 1, 2))
+
+    def redo_row(f, j):
+        for h in range(2):
+            for x in (0, 64):
+                redo(f, j, h, x, 64)
+
+    pl.when(last)(lambda: redo_row(0, 3))
+    pl.when(first)(lambda: redo_row(2, 0))
+    for j in range(4):
+        for h in range(2):
+            redo(0, j, h, SIDE - 8, 8)
+            redo(2, j, h, 0, 8)
+            if j:
+                turned[pl.ds(slot(0, j, h) - j, j), :] = turned[
+                    pl.ds(slot(0, j, h) + SIDE - j, j), :]
+    pack_1(3, 31)
+    recv[1, me] = send[1, me]
+    send_family(0)
+    pl.when(me != ALL - 1)(
+        push(
+            send.at[1, ALL - 1], recv.at[1, me], send_sem.at[1], recv_sem.at[1], 3, 31
+        ).start)
 
     c = me
     def coeff(ref, k):
@@ -330,6 +399,52 @@
         back_recv[g, me] = back_send[g, me]
         dispatch(
             face, sub, back_send.at[g], back_recv.at[g], send_sem.at[3 + g], recv_sem.at[3 + g])
+
+    block_row = 4 * lax.broadcasted_iota(jnp.int32, (8, 8, LANES), 0) + (
+        lax.broadcasted_iota(jnp.int32, (8, 8, LANES), 1) // 2)
+
+    for g in (2, 1):
+        arrive(g)
+
+        def unpack(b, carry, g=g):
+            at = pl.multiple_of(8 * b, 8)
+            i = (3 - (b >> 2)) * 32 + 8 * (b & 3)
+            rows = recv[g, pl.ds(i, 8)].astype(jnp.float32)
+            if g == 2:
+                before = recv[g, pl.ds((i + 96) & (ALL - 1), 8)].astype(jnp.float32)
+                rows = jnp.where(block_row + 32 * (b & 3) > c, before, rows)
+            chain[pl.ds(at + 3, 8)] = rows
+            return carry
+
+        lax.fori_loop(0, 16, unpack, 0, unroll=2)
+        for e in range(3):
+            chain[e] = chain[ALL + e]
+            chain[ALL + 3 + e] = chain[3 + e]
+
+        def stencil_ring(b, carry, g=g):
+            at = 8 * b
+            i = (3 - (b >> 2)) * 32 + 8 * (b & 3)
+            window = [chain[at + n] for n in range(14)]
+            for n in range(8):
+                total = blend(window[n : n + 7][::-1])
+                if g == 1:
+                    back_send[g, i + n] = total.astype(jnp.bfloat16)
+                else:
+                    ring[i + n] = total
+            return carry
+
+        lax.fori_loop(0, 16, stencil_ring, 0)
+        if g == 2:
+
+            def regroup(b, carry):
+                rows = ring[pl.ds(8 * b, 8)]
+                after = ring[pl.ds((8 * b + 32) & (ALL - 1), 8)]
+                back_send[2, pl.ds(8 * b, 8)] = jnp.where(
+                    block_row + 32 * (b & 3) > c, after, rows).astype(jnp.bfloat16)
+                return carry
+
+            lax.fori_loop(0, 16, regroup, 0, unroll=2)
+        depart(g)
 
     arrive(0)
 
@@ -370,52 +485,6 @@
         back_send[0, pl.ds(32 * q, 32)] = (
             jnp.where(row_256 > c, from_n, from_s).reshape(32, 8, LANES).astype(jnp.bfloat16))
     depart(0)
-
-    block_row = 4 * lax.broadcasted_iota(jnp.int32, (8, 8, LANES), 0) + (
-        lax.broadcasted_iota(jnp.int32, (8, 8, LANES), 1) // 2)
-
-    for g in (1, 2):
-        arrive(g)
-
-        def unpack(b, carry, g=g):
-            at = pl.multiple_of(8 * b, 8)
-            i = (3 - (b >> 2)) * 32 + 8 * (b & 3)
-            rows = recv[g, pl.ds(i, 8)].astype(jnp.float32)
-            if g == 2:
-                before = recv[g, pl.ds((i + 96) & (ALL - 1), 8)].astype(jnp.float32)
-                rows = jnp.where(block_row + 32 * (b & 3) > c, before, rows)
-            chain[pl.ds(at + 3, 8)] = rows
-            return carry
-
-        lax.fori_loop(0, 16, unpack, 0, unroll=2)
-        for e in range(3):
-            chain[e] = chain[ALL + e]
-            chain[ALL + 3 + e] = chain[3 + e]
-
-        def stencil_ring(b, carry, g=g):
-            at = 8 * b
-            i = (3 - (b >> 2)) * 32 + 8 * (b & 3)
-            window = [chain[at + n] for n in range(14)]
-            for n in range(8):
-                total = blend(window[n : n + 7][::-1])
-                if g == 1:
-                    back_send[g, i + n] = total.astype(jnp.bfloat16)
-                else:
-                    ring[i + n] = total
-            return carry
-
-        lax.fori_loop(0, 16, stencil_ring, 0)
-        if g == 2:
-
-            def regroup(b, carry):
-                rows = ring[pl.ds(8 * b, 8)]
-                after = ring[pl.ds((8 * b + 32) & (ALL - 1), 8)]
-                back_send[2, pl.ds(8 * b, 8)] = jnp.where(
-                    block_row + 32 * (b & 3) > c, after, rows).astype(jnp.bfloat16)
-                return carry
-
-            lax.fori_loop(0, 16, regroup, 0, unroll=2)
-        depart(g)
 
     gain = gain_ref[...]
     scale = ls_ref[...]
@@ -440,12 +509,12 @@
             upper, field_ref[high[g], j].astype(jnp.float32), field_ref[low[g], j].astype(jnp.float32))
         result = source + scale * branch
         for f, kept in ((high[g], upper), (low[g], jnp.logical_not(upper))):
-            seen = (g, f) in ((1, 0), (2, 1), (2, 2))
+            seen = (g, f) in ((1, 1), (0, 0), (0, 2))
             row = jnp.where(kept, result, out_ref[f, j].astype(jnp.float32)) if seen else result
             out_ref[f, j] = row.astype(jnp.bfloat16)
         return carry
 
-    for g in range(3):
+    for g in (2, 1, 0):
         all_blocks(
             face, sub, back_send.at[g], back_recv.at[g], send_sem.at[3 + g], recv_sem.at[3 + g]
         ).wait_recv()
@@ -465,6 +534,8 @@
 
     for cond, copy in inner:
         pl.when(cond)(copy.wait_send)
+    for copy in outer:
+        copy.wait_send()
     pl.when(first | last)(
         lambda: push(pieces, pieces, piece_sent, piece_sem.at[0], face, sub).wait_send())
     for g in range(3):
@@ -522,6 +593,7 @@
             blocks,
             dma((6,)),
             dma((6,)),
+            pltpu.SemaphoreType.REGULAR((2,)),
             dma((2, 3)),
             dma((3,)),
             dma((3,)),

time: 43.3 us -> 39.3 us (0.908)
  Pallas kernels: 42.4 us -> 38.3 us
    pallas_call x1, Pallas kernels: 42.4 us -> 38.3 us  [run(): pl.pallas_call(kernel, out_shape=jax.ShapeDtypeStruct(field.shape, jnp.bf...]
where the time goes in v5:
time: 39.3 us; the launch traced here: 39.2 us
  Pallas kernels  38.3 us (97%)
  local copies, waits for them, and re-layouts  0.88 us (2%)
    pallas_call x1, Pallas kernels, run(): pl.pallas_call(kernel, out_shape=jax.ShapeDtypeStruct(field.shape, jnp.bf...  38.3 us
    unnamed x1, local copies, waits for them, and re-layouts  0.88 us

profile of v5, /device:TPU:1, one launch (start us, length us, event | category | flops | bytes accessed | tf_op | source)
XLA Modules:
  0.0 39.2 jit_solution(6466540840987158987)
XLA Ops:
  0.0 38.3 %shard_map.91 = bf16[3,4,128,256]{3,2,1,0:T(8,128)(2,1)S(1)} custom-call(bf16[3,4,128,256]{3,2,1,0:T(8,128)(2,1)} %bitcast.9, f32[9,256]{1,0:T(8,128)} %dwk_hbm.1, f32[1,256]{1,0:T(1,128)} %bitcast.10, f32[7,256]{1,0:T(8,128)} %zk_hbm.1, f32[1,256]{1,0:T(1,128)} %bitcast.11, f32[1,256]{1,0:T(1,128)} %bitcast.12, bf16[256,768]{1,0:T(8,128)(2,1)} %w_in_hbm.1, ...), custom_call_target="tpu_custom_call" | custom-call | tf_op jit(solution)/shard_map/pallas_call | solution.py:556
  38.3 0.9 %copy.12 = bf16[3,1,4,128,256]{4,3,2,1,0:T(8,128)(2,1)} copy(bf16[3,1,4,128,256]{4,3,2,1,0:T(8,128)(2,1)S(1)} %bitcast.8) | data formatting | bytes 1572864

commit v6 on v5

--- a/solution.py
+++ b/solution.py
@@ -22,12 +22,29 @@
 LIN_BLOCKS = 17
 
 
-def peer_at(face, sub, step):
-    pf = (face + step) & 3
-    px = ((sub >> 3) + (step >> 2)) & 3
-    pz = ((sub >> 1) + (step >> 4)) & 3
-    pc = (sub + (step >> 6)) & 1
-    return pf, (px << 3) + (pz << 1) + pc
+def hops(step):
+    return sum(min(d, 4 - d) for d in step[:3])
+
+
+STEPS = sorted(
+    (
+        (face, x, z, core)
+        for face in range(4)
+        for x in range(4)
+        for z in range(4)
+        for core in range(2)
+        if face + x + z + core
+    ),
+    key=lambda step: -hops(step),
+)
+
+
+def peers(face, sub):
+    for df, dx, dz, dc in STEPS:
+        px = ((sub >> 3) + dx) & 3
+        pz = ((sub >> 1) + dz) & 3
+        pc = (sub + dc) & 1
+        yield (face + df) & 3, (px << 3) + (pz << 1) + pc
 
 
 def greet(sem, pf, ps):
@@ -78,22 +95,19 @@
         else:
             pl.when(pf * 32 + ps != later)(copy.start)
 
-    def step(i, carry):
-        pf, ps = peer_at(face, sub, ALL - i)
+    waiting = None
+    for pf, ps in peers(face, sub):
         prepare(pf, ps)
-        push(*carry)
-        return pf, ps
-
-    pf, ps = peer_at(face, sub, ALL - 1)
-    prepare(pf, ps)
-    push(*lax.fori_loop(2, ALL, step, (pf, ps), unroll=2))
+        if waiting is not None:
+            push(*waiting)
+        waiting = pf, ps
+    push(*waiting)
 
 
 def dispatch(face, sub, source, target, send_sem, recv_sem):
     me = face * 32 + sub
 
-    def step(i, carry):
-        pf, ps = peer_at(face, sub, ALL - i)
+    for pf, ps in peers(face, sub):
         pltpu.make_async_remote_copy(
             source.at[pf * 32 + ps],
             target.at[me],
@@ -102,9 +116,6 @@
             device_id=(pf, ps),
             device_id_type=MESH,
         ).start()
-        return carry
-
-    lax.fori_loop(1, ALL, step, 0, unroll=2)
 
 
 def all_blocks(face, sub, source, target, send_sem, recv_sem):
@@ -144,10 +155,47 @@
     partners = announce(face, sub)
     for load in loads[1:]:
         load.start()
-    loads[0].wait()
 
     def start(f, r, h=0):
         return (f * 12 + r * 2 + h) * PITCH + ROW
+
+    def push(source, target, sent, got, pf, ps):
+        return pltpu.make_async_remote_copy(
+            source, target, sent, got, device_id=(pf, ps), device_id_type=MESH
+        )
+
+    rows = []
+    for f in (2, 1, 0):
+        rows.append((sub < 31, push(
+            field_hbm.at[f, 3], row_lo.at[f], row_sent.at[0, f], lo_sem.at[f], face, sub + 1)))
+        rows.append((sub > 0, push(
+            field_hbm.at[f, 0], row_hi.at[f], row_sent.at[1, f], hi_sem.at[f], face, sub - 1)))
+        if f:
+            rows.append((last, push(
+                field_hbm.at[f, 3], row_lo.at[f - 1], row_sent.at[0, f], lo_sem.at[f - 1],
+                west if f == 1 else face, 0)))
+        if f < 2:
+            rows.append((first, push(
+                field_hbm.at[f, 0], row_hi.at[f + 1], row_sent.at[1, f], hi_sem.at[f + 1],
+                east if f == 0 else face, 31)))
+    sides = []
+    for d, cond in ((-1, sub > 0), (0, sub >= 0), (1, sub < 31)):
+        sides.append((cond, push(
+            cols.at[0], left1.at[1 - d], col_sent.at[0, 1 - d], left_sem.at[1 - d], east, sub + d)))
+        sides.append((cond, push(
+            cols.at[1], right2.at[1 - d], col_sent.at[1, 1 - d], right_sem.at[1 - d], west, sub + d)))
+    outer = []
+    outer.append(push(
+        cols.at[2], rim_hi.at[sub], rim_sent.at[0], rim_sem.at[0], east, 31))
+    outer.append(push(
+        cols.at[3], rim_lo.at[sub], rim_sent.at[1], rim_sem.at[1], west, 0))
+
+    pl.semaphore_wait(pltpu.get_barrier_semaphore(), partners)
+    for cond, copy in rows:
+        pl.when(cond)(copy.start)
+    for n in range(1, 4):
+        greet(round_sem.at[0], face, (sub + 8 * n) & 31)
+    loads[0].wait()
 
     def widen(t, carry):
         f = t >> 2
@@ -173,43 +221,11 @@
 
     pl.when(last)(lambda: cut(start(0, 4)))
     pl.when(first)(lambda: cut(start(2, 1)))
-
-    def push(source, target, sent, got, pf, ps):
-        return pltpu.make_async_remote_copy(
-            source, target, sent, got, device_id=(pf, ps), device_id_type=MESH
-        )
-
-    inner = []
-    for f in range(3):
-        inner.append((sub < 31, push(
-            field_ref.at[f, 3], row_lo.at[f], row_sent.at[0, f], lo_sem.at[f], face, sub + 1)))
-        inner.append((sub > 0, push(
-            field_ref.at[f, 0], row_hi.at[f], row_sent.at[1, f], hi_sem.at[f], face, sub - 1)))
-    inner.append((last, push(
-        field_ref.at[1, 3], row_lo.at[0], row_sent.at[0, 1], lo_sem.at[0], west, 0)))
-    inner.append((last, push(
-        field_ref.at[2, 3], row_lo.at[1], row_sent.at[0, 2], lo_sem.at[1], face, 0)))
-    inner.append((first, push(
-        field_ref.at[0, 0], row_hi.at[1], row_sent.at[1, 0], hi_sem.at[1], east, 31)))
-    inner.append((first, push(
-        field_ref.at[1, 0], row_hi.at[2], row_sent.at[1, 1], hi_sem.at[2], face, 31)))
-    for d, cond in ((-1, sub > 0), (0, sub >= 0), (1, sub < 31)):
-        inner.append((cond, push(
-            cols.at[0], left1.at[1 - d], col_sent.at[0, 1 - d], left_sem.at[1 - d], east, sub + d)))
-        inner.append((cond, push(
-            cols.at[1], right2.at[1 - d], col_sent.at[1, 1 - d], right_sem.at[1 - d], west, sub + d)))
-    outer = []
-    outer.append(push(
-        cols.at[2], rim_hi.at[sub], rim_sent.at[0], rim_sem.at[0], east, 31))
-    outer.append(push(
-        cols.at[3], rim_lo.at[sub], rim_sent.at[1], rim_sem.at[1], west, 0))
-
-    pl.semaphore_wait(pltpu.get_barrier_semaphore(), partners)
-    for cond, copy in inner:
+    for cond, copy in sides:
         pl.when(cond)(copy.start)
+    pl.semaphore_wait(round_sem.at[0], 3)
     for n in range(1, 4):
-        greet(round_sem.at[0], face, (sub + 8 * n) & 31)
-
+        greet(round_sem.at[1], (face + n) & 3, sub)
     for load in loads[1:]:
         load.wait()
 
@@ -236,11 +252,7 @@
                         zero, f, j, h, x, 56, rows)
         return carry
 
-    inside(0, 0)
-    pl.semaphore_wait(round_sem.at[0], 3)
-    for n in range(1, 4):
-        greet(round_sem.at[1], (face + n) & 3, sub)
-    lax.fori_loop(1, 3, inside, 0)
+    lax.fori_loop(0, 3, inside, 0)
     pl.semaphore_wait(round_sem.at[1], 3)
     for copy in outer:
         copy.start()
@@ -258,58 +270,69 @@
     def took(ref, sem):
         push(ref, ref, row_sent.at[0, 0], sem, face, sub).wait_recv()
 
-    for f in range(3):
-        pl.when((sub > 0) if f == 2 else (sub >= 0))(
-            lambda f=f: took(row_lo.at[f], lo_sem.at[f]))
-        pl.when((sub < 31) if f == 0 else (sub >= 0))(
-            lambda f=f: took(row_hi.at[f], hi_sem.at[f]))
-    for e, cond in ((0, sub > 0), (1, sub >= 0), (2, sub < 31)):
-        pl.when(cond)(lambda e=e: took(left1.at[e], left_sem.at[e]))
-        pl.when(cond)(lambda e=e: took(right2.at[e], right_sem.at[e]))
-
-    for f in range(3):
+    def fill(f):
+        pl.when((sub > 0) if f == 2 else (sub >= 0))(lambda: took(row_lo.at[f], lo_sem.at[f]))
+        pl.when((sub < 31) if f == 0 else (sub >= 0))(lambda: took(row_hi.at[f], hi_sem.at[f]))
         for h in range(2):
             half = slice(h * LANES, (h + 1) * LANES)
             grid[pl.ds(start(f, 0, h), SIDE), :] = row_lo[f, :, half].astype(jnp.float32)
             grid[pl.ds(start(f, 5, h), SIDE), :] = row_hi[f, :, half].astype(jnp.float32)
 
-    for r, size in ((0, 8), (4, 4)):
-        grid[pl.ds(start(0, r) - 1, size, stride=PITCH), :] = grid[
-            pl.ds(start(1, r) + SIDE - 1, size, stride=PITCH), :]
-        grid[pl.ds(start(1, r) + SIDE, size, stride=PITCH), :] = grid[
-            pl.ds(start(0, r), size, stride=PITCH), :]
-    for f, x, ref in ((1, -1, left1), (2, SIDE, right2)):
+    def side(f, x, ref, sem):
+        for e, cond in ((0, sub > 0), (1, sub >= 0), (2, sub < 31)):
+            pl.when(cond)(lambda e=e: took(ref.at[e], sem.at[e]))
         before = ref[0].astype(jnp.float32)
         after = ref[2].astype(jnp.float32)
         grid[pl.ds(start(f, 0) + x, 2, stride=PITCH), :] = before[6:8]
         grid[pl.ds(start(f, 1) + x, 8, stride=PITCH), :] = ref[1].astype(jnp.float32)
         grid[pl.ds(start(f, 5) + x, 2, stride=PITCH), :] = after[0:2]
-    def corners(r):
-        for f in range(3):
+
+    def next_to(f, x, other, at):
+        for r, size in ((0, 8), (4, 4)):
+            grid[pl.ds(start(f, r) + x, size, stride=PITCH), :] = grid[
+                pl.ds(start(other, r) + at, size, stride=PITCH), :]
+
+    def corners(f):
+        def clear(r):
             for x in (-1, SIDE):
-                grid[pl.ds(start(f, r) + x, 2, stride=PITCH), :] = jnp.zeros((2, LANES), jnp.float32)
-
-    pl.when(first)(lambda: corners(0))
-    pl.when(last)(lambda: corners(5))
-
-    def around(f, carry):
+                grid[pl.ds(start(f, r) + x, 2, stride=PITCH), :] = jnp.zeros(
+                    (2, LANES), jnp.float32)
+
+        pl.when(first)(lambda: clear(0))
+        pl.when(last)(lambda: clear(5))
+
+    def redo(f, j, h, x, size):
+        total = jnp.broadcast_to(weight(dwb_ref, 0, h), (size, LANES))
+        turned[pl.ds(slot(f, j, h) + x, size), :] = partial_sum(
+            total, f, j, h, x, size, (0, 1, 2))
+
+    def wrap(f):
+        for j in range(1, 4):
+            for h in range(2):
+                turned[pl.ds(slot(f, j, h) - j, j), :] = turned[
+                    pl.ds(slot(f, j, h) + SIDE - j, j), :]
+
+    def around(f):
         for j in range(4):
             for h in range(2):
                 for x in (0, SIDE - 8):
-                    zero = jnp.broadcast_to(weight(dwb_ref, 0, h), (8, LANES))
-                    turned[pl.ds(slot(f, j, h) + x, 8), :] = partial_sum(
-                        zero, f, j, h, x, 8, (0, 1, 2))
+                    redo(f, j, h, x, 8)
                 if j in (0, 3):
                     for x in (8, 64):
                         at = pl.ds(slot(f, j, h) + x, 56)
                         turned[at, :] = partial_sum(
                             turned[at, :], f, j, h, x, 56, (0,) if j == 0 else (2,))
-                if j:
-                    turned[pl.ds(slot(f, j, h) - j, j), :] = turned[
-                        pl.ds(slot(f, j, h) + SIDE - j, j), :]
-        return carry
-
-    lax.fori_loop(0, 3, around, 0)
+        wrap(f)
+
+    side(2, SIDE, right2, right_sem)
+    side(1, -1, left1, left_sem)
+    fill(2)
+    corners(2)
+    around(2)
+    fill(1)
+    next_to(1, SIDE, 0, 0)
+    corners(1)
+    around(1)
 
     high = (0, 1, 2)
     low = (2, 0, 1)
@@ -330,6 +353,16 @@
         return pack
 
     send_family(2)
+    fill(0)
+    next_to(0, -1, 1, SIDE - 1)
+    next_to(1, SIDE, 0, 0)
+    corners(0)
+    corners(1)
+    around(0)
+    for j in (0, 3):
+        for h in range(2):
+            redo(1, j, h, SIDE - 8, 8)
+    wrap(1)
     pack_1 = send_family(1, ALL - 1)
 
     def rim(ref, sem, f, r):
@@ -347,13 +380,8 @@
         for h in range(2):
             grid[pl.ds(start(f, 0, h) + x, 6, stride=2 * PITCH), :] = ref[h].astype(jnp.float32)[:6]
 
-    pl.when(first)(lambda: corners(0))
-    pl.when(last)(lambda: corners(5))
-
-    def redo(f, j, h, x, size):
-        total = jnp.broadcast_to(weight(dwb_ref, 0, h), (size, LANES))
-        turned[pl.ds(slot(f, j, h) + x, size), :] = partial_sum(
-            total, f, j, h, x, size, (0, 1, 2))
+    corners(0)
+    corners(2)
 
     def redo_row(f, j):
         for h in range(2):
@@ -366,9 +394,7 @@
         for h in range(2):
             redo(0, j, h, SIDE - 8, 8)
             redo(2, j, h, 0, 8)
-            if j:
-                turned[pl.ds(slot(0, j, h) - j, j), :] = turned[
-                    pl.ds(slot(0, j, h) + SIDE - j, j), :]
+    wrap(0)
     pack_1(3, 31)
     recv[1, me] = send[1, me]
     send_family(0)
@@ -530,9 +556,9 @@
             for h in range(2):
                 turned[pl.ds(slot(g, j, h) + SIDE - j, j), :] = turned[
                     pl.ds(slot(g, j, h) - j, j), :]
-        lax.fori_loop(0, 4, functools.partial(mlp, g), 0)
-
-    for cond, copy in inner:
+        lax.fori_loop(0, 4, functools.partial(mlp, g), 0, unroll=4)
+
+    for cond, copy in rows + sides:
         pl.when(cond)(copy.wait_send)
     for copy in outer:
         copy.wait_send()

time: 39.3 us -> 36.3 us (0.924)
  Pallas kernels: 38.3 us -> 35.3 us
    pallas_call x1, Pallas kernels: 38.3 us -> 35.3 us  [run(): pl.pallas_call(kernel, out_shape=jax.ShapeDtypeStruct(field.shape, jnp.bf...]
where the time goes in v6:
time: 36.3 us; the launch traced here: 36.2 us
  Pallas kernels  35.3 us (97%)
  local copies, waits for them, and re-layouts  0.88 us (2%)
    pallas_call x1, Pallas kernels, run(): pl.pallas_call(kernel, out_shape=jax.ShapeDtypeStruct(field.shape, jnp.bf...  35.3 us
    unnamed x1, local copies, waits for them, and re-layouts  0.88 us

profile of v6, /device:TPU:1, one launch (start us, length us, event | category | flops | bytes accessed | tf_op | source)
XLA Modules:
  0.0 36.2 jit_solution(2936710679257895459)
XLA Ops:
  0.0 35.3 %shard_map.91 = bf16[3,4,128,256]{3,2,1,0:T(8,128)(2,1)S(1)} custom-call(bf16[3,4,128,256]{3,2,1,0:T(8,128)(2,1)} %bitcast.9, f32[9,256]{1,0:T(8,128)} %dwk_hbm.1, f32[1,256]{1,0:T(1,128)} %bitcast.10, f32[7,256]{1,0:T(8,128)} %zk_hbm.1, f32[1,256]{1,0:T(1,128)} %bitcast.11, f32[1,256]{1,0:T(1,128)} %bitcast.12, bf16[256,768]{1,0:T(8,128)(2,1)} %w_in_hbm.1, ...), custom_call_target="tpu_custom_call" | custom-call | tf_op jit(solution)/shard_map/pallas_call | solution.py:582
  35.3 0.9 %copy.12 = bf16[3,1,4,128,256]{4,3,2,1,0:T(8,128)(2,1)} copy(bf16[3,1,4,128,256]{4,3,2,1,0:T(8,128)(2,1)S(1)} %bitcast.8) | data formatting | bytes 1572864

commit v7 on v6

--- a/solution.py
+++ b/solution.py
@@ -78,7 +78,7 @@
     return 17 + inner_edge.astype(jnp.int32)
 
 
-def exchange(face, sub, prepare, source, target, send_sem, recv_sem, later=None):
+def exchange(face, sub, prepare, source, target, send_sem, recv_sem, ready=None):
     me = face * 32 + sub
 
     def push(pf, ps):
@@ -90,10 +90,10 @@
             device_id=(pf, ps),
             device_id_type=MESH,
         )
-        if later is None:
+        if ready is None:
             copy.start()
         else:
-            pl.when(pf * 32 + ps != later)(copy.start)
+            pl.when(ready(pf * 32 + ps))(copy.start)
 
     waiting = None
     for pf, ps in peers(face, sub):
@@ -191,10 +191,10 @@
         cols.at[3], rim_lo.at[sub], rim_sent.at[1], rim_sem.at[1], west, 0))
 
     pl.semaphore_wait(pltpu.get_barrier_semaphore(), partners)
+    for n in range(1, 4):
+        greet(round_sem.at[0], face, (sub + 8 * n) & 31)
     for cond, copy in rows:
         pl.when(cond)(copy.start)
-    for n in range(1, 4):
-        greet(round_sem.at[0], face, (sub + 8 * n) & 31)
     loads[0].wait()
 
     def widen(t, carry):
@@ -206,9 +206,24 @@
             ].astype(jnp.float32)
         return carry
 
-    lax.fori_loop(0, 12, widen, 0)
-    for n, (f, x) in enumerate(((2, SIDE - 1), (1, 0), (0, SIDE - 1), (2, 0))):
+    for f, x in ((2, SIDE - 16), (1, 0)):
+        for j in range(4):
+            for h in range(2):
+                grid[pl.ds(start(f, j + 1, h) + x, 16), :] = field_ref[
+                    f, j, x : x + 16, h * LANES : (h + 1) * LANES
+                ].astype(jnp.float32)
+
+    def column(n, f, x):
         cols[n] = grid[pl.ds(start(f, 1) + x, 8, stride=PITCH), :].astype(jnp.bfloat16)
+
+    column(0, 2, SIDE - 1)
+    column(1, 1, 0)
+    lax.fori_loop(0, 6, widen, 0)
+    for cond, copy in sides:
+        pl.when(cond)(copy.start)
+    lax.fori_loop(6, 12, widen, 0)
+    column(2, 0, SIDE - 1)
+    column(3, 2, 0)
 
     def cut(base):
         def one(t, carry):
@@ -221,11 +236,6 @@
 
     pl.when(last)(lambda: cut(start(0, 4)))
     pl.when(first)(lambda: cut(start(2, 1)))
-    for cond, copy in sides:
-        pl.when(cond)(copy.start)
-    pl.semaphore_wait(round_sem.at[0], 3)
-    for n in range(1, 4):
-        greet(round_sem.at[1], (face + n) & 3, sub)
     for load in loads[1:]:
         load.wait()
 
@@ -252,7 +262,11 @@
                         zero, f, j, h, x, 56, rows)
         return carry
 
-    lax.fori_loop(0, 3, inside, 0)
+    inside(2, 0)
+    pl.semaphore_wait(round_sem.at[0], 3)
+    for n in range(1, 4):
+        greet(round_sem.at[1], (face + n) & 3, sub)
+    lax.fori_loop(0, 2, inside, 0)
     pl.semaphore_wait(round_sem.at[1], 3)
     for copy in outer:
         copy.start()
@@ -338,7 +352,7 @@
     low = (2, 0, 1)
     row_in = lax.broadcasted_iota(jnp.int32, (8, LANES), 0) // 2
 
-    def send_family(g, later=None):
+    def send_family(g, ready=None):
         def pack(pf, ps):
             c = pf * 32 + ps
             t = (c - 4 * sub) & (ALL - 1)
@@ -347,7 +361,7 @@
             send[g, c] = jnp.where(row_in + 4 * sub > c, above, below).astype(jnp.bfloat16)
 
         exchange(
-            face, sub, pack, send.at[g], recv.at[g], send_sem.at[g], recv_sem.at[g], later)
+            face, sub, pack, send.at[g], recv.at[g], send_sem.at[g], recv_sem.at[g], ready)
         pack(face, sub)
         recv[g, me] = send[g, me]
         return pack
@@ -363,7 +377,8 @@
         for h in range(2):
             redo(1, j, h, SIDE - 8, 8)
     wrap(1)
-    pack_1 = send_family(1, ALL - 1)
+    rim_device = first | last
+    pack_1 = send_family(1, lambda owner: (owner != ALL - 1) | ~rim_device)
 
     def rim(ref, sem, f, r):
         took(ref, sem)
@@ -393,15 +408,21 @@
     for j in range(4):
         for h in range(2):
             redo(0, j, h, SIDE - 8, 8)
+    wrap(0)
+
+    def pack_last():
+        pack_1(3, 31)
+        recv[1, me] = send[1, me]
+
+    pl.when(rim_device)(pack_last)
+    for j in range(4):
+        for h in range(2):
             redo(2, j, h, 0, 8)
-    wrap(0)
-    pack_1(3, 31)
-    recv[1, me] = send[1, me]
-    send_family(0)
-    pl.when(me != ALL - 1)(
+    pl.when(rim_device & (me != ALL - 1))(
         push(
             send.at[1, ALL - 1], recv.at[1, me], send_sem.at[1], recv_sem.at[1], 3, 31
         ).start)
+    send_family(0)
 
     c = me
     def coeff(ref, k):

time: 36.3 us -> 36.2 us (level)
  no operation moved by 1% of the time
where the time goes in v7:
time: 36.2 us; the launch traced here: 36.1 us
  Pallas kernels  35.2 us (97%)
  local copies, waits for them, and re-layouts  0.88 us (2%)
    pallas_call x1, Pallas kernels, run(): pl.pallas_call(kernel, out_shape=jax.ShapeDtypeStruct(field.shape, jnp.bf...  35.2 us
    unnamed x1, local copies, waits for them, and re-layouts  0.88 us

profile of v7, /device:TPU:1, one launch (start us, length us, event | category | flops | bytes accessed | tf_op | source)
XLA Modules:
  0.0 36.1 jit_solution(13409698727085528095)
XLA Ops:
  0.0 35.2 %shard_map.91 = bf16[3,4,128,256]{3,2,1,0:T(8,128)(2,1)S(1)} custom-call(bf16[3,4,128,256]{3,2,1,0:T(8,128)(2,1)} %bitcast.9, f32[9,256]{1,0:T(8,128)} %dwk_hbm.1, f32[1,256]{1,0:T(1,128)} %bitcast.10, f32[7,256]{1,0:T(8,128)} %zk_hbm.1, f32[1,256]{1,0:T(1,128)} %bitcast.11, f32[1,256]{1,0:T(1,128)} %bitcast.12, bf16[256,768]{1,0:T(8,128)(2,1)} %w_in_hbm.1, ...), custom_call_target="tpu_custom_call" | custom-call | tf_op jit(solution)/shard_map/pallas_call | solution.py:603
  35.2 0.9 %copy.12 = bf16[3,1,4,128,256]{4,3,2,1,0:T(8,128)(2,1)} copy(bf16[3,1,4,128,256]{4,3,2,1,0:T(8,128)(2,1)S(1)} %bitcast.8) | data formatting | bytes 1572864

commit v8 on v7

--- a/solution.py
+++ b/solution.py
@@ -35,7 +35,7 @@
         for core in range(2)
         if face + x + z + core
     ),
-    key=lambda step: -hops(step),
+    key=lambda step: (-hops(step) - 3 * (step[3] == 0)),
 )
 
 

time: 36.2 us -> 36.1 us (level)
  no operation moved by 1% of the time
where the time goes in v8:
time: 36.1 us; the launch traced here: 36 us
  Pallas kernels  35.1 us (97%)
  local copies, waits for them, and re-layouts  0.88 us (2%)
    pallas_call x1, Pallas kernels, run(): pl.pallas_call(kernel, out_shape=jax.ShapeDtypeStruct(field.shape, jnp.bf...  35.1 us
    unnamed x1, local copies, waits for them, and re-layouts  0.88 us

profile of v8, /device:TPU:1, one launch (start us, length us, event | category | flops | bytes accessed | tf_op | source)
XLA Modules:
  0.0 36.0 jit_solution(9435103440168017496)
XLA Ops:
  0.0 35.1 %shard_map.91 = bf16[3,4,128,256]{3,2,1,0:T(8,128)(2,1)S(1)} custom-call(bf16[3,4,128,256]{3,2,1,0:T(8,128)(2,1)} %bitcast.9, f32[9,256]{1,0:T(8,128)} %dwk_hbm.1, f32[1,256]{1,0:T(1,128)} %bitcast.10, f32[7,256]{1,0:T(8,128)} %zk_hbm.1, f32[1,256]{1,0:T(1,128)} %bitcast.11, f32[1,256]{1,0:T(1,128)} %bitcast.12, bf16[256,768]{1,0:T(8,128)(2,1)} %w_in_hbm.1, ...), custom_call_target="tpu_custom_call" | custom-call | tf_op jit(solution)/shard_map/pallas_call | solution.py:603
  35.1 0.9 %copy.12 = bf16[3,1,4,128,256]{4,3,2,1,0:T(8,128)(2,1)} copy(bf16[3,1,4,128,256]{4,3,2,1,0:T(8,128)(2,1)S(1)} %bitcast.8) | data formatting | bytes 1572864
